TPU v7x, 256 devices: a whole 4x4x8 slice. The times are simulated.
256 devices in a mesh: session: 8 (over x_lo, y), ctx: 32 (over x_hi, z, core).
Axes of the slice: x: 4 (x_hi: 2, x_lo: 2; x = x_hi * 2 + x_lo), y: 4, z: 8, core: 2. Of those that a mesh axis runs over, the one named last changes fastest.
Arguments:
- frames: float32 [49152, 1024], P(('session', 'ctx')), parts along dimension 0, may hold values from -6 to 6
- attend_gain: float32 [1024], replicated, may hold values from 0.25 to 1.75
- query_weight: bfloat16 [1024, 1024], replicated, may hold values from -8 to 8
- key_weight: bfloat16 [1024, 1024], replicated, may hold values from -8 to 8
- value_weight: bfloat16 [1024, 1024], replicated, may hold values from -0.1875 to 0.1875
- output_weight: bfloat16 [1024, 1024], replicated, may hold values from -0.1875 to 0.1875
- mixer_gain: float32 [1024], replicated, may hold values from 0.25 to 1.75
- depthwise: float32 [31, 1024], replicated, may hold values from -1 to 1
- mixer_bias: float32 [1024], replicated, may hold values from -3 to 3
Outputs:
- block_out: float32 [49152, 1024], P(('session', 'ctx')), parts along dimension 0
There are 8 independent parts, one for each index of `session`. A program takes and returns all parts, laid end to end along the dimension named above; an argument that names none is the same for every part. Nothing has to cross between parts.
All inputs are finite; a program needn't handle non-finite values.
Results may differ from a plain program's by a relative error of at most 0.0031.
Values may be sent and summed in bfloat16 or wider, within the bound.
A program may use at most 256 MiB of HBM per device.

v0:
```python
import jax
import jax.numpy as jnp
from jax import lax
from jax.sharding import PartitionSpec as P

HEADS = 16
KERNEL = 31


def with_halo(block, sides, width):
    for axis, dim in sides:
        count = lax.axis_size(axis)
        forward = [(i, i + 1) for i in range(count - 1)]
        backward = [(target, source) for source, target in forward]
        low = lax.ppermute(
            lax.slice_in_dim(block, block.shape[dim] - width, None, axis=dim), axis, forward
        )
        high = lax.ppermute(lax.slice_in_dim(block, 0, width, axis=dim), axis, backward)
        block = jnp.concatenate([low, block, high], axis=dim)
    return block


def norm_rows(values_in, gain):
    center = jnp.mean(values_in, axis=1, keepdims=True)
    spread = jnp.mean(jnp.square(values_in - center), axis=1, keepdims=True)
    return (values_in - center) * lax.rsqrt(spread + 1e-05) * gain


def project(source, weight):
    return jnp.dot(source, weight, preferred_element_type=jnp.float32).astype(jnp.bfloat16)


def per_device(
    frames,
    attend_gain,
    query_weight,
    key_weight,
    value_weight,
    output_weight,
    mixer_gain,
    depthwise,
    mixer_bias,
):
    row_count, feature_count = frames.shape
    head_size = feature_count // HEADS
    score_scale = head_size ** (-0.5)
    normed = norm_rows(frames, attend_gain).astype(jnp.bfloat16)
    query_heads = project(normed, query_weight).reshape(row_count, HEADS, head_size)
    key_rows = project(normed, key_weight)
    value_rows = project(normed, value_weight)
    key_block = lax.all_gather(key_rows, "ctx", axis=0, tiled=True)
    highest = jnp.full((HEADS, row_count), -1e30, jnp.float32)
    block_rows = key_block.shape[0]
    key_heads = key_block.reshape(block_rows, HEADS, head_size)
    value_heads = lax.all_gather(value_rows, "ctx", axis=0, tiled=True).reshape(
        block_rows, HEADS, head_size
    )
    scores = (
        jnp.einsum("qhd,khd->hqk", query_heads, key_heads, preferred_element_type=jnp.float32)
        * score_scale
    )
    new_high = jnp.maximum(highest, jnp.max(scores, axis=2))
    weights = jnp.exp(scores - new_high[:, :, None])
    partial_sum = jnp.einsum(
        "hqk,khd->qhd",
        weights.astype(jnp.bfloat16),
        value_heads,
        preferred_element_type=jnp.float32,
    )
    totals = jnp.sum(weights, axis=2)
    running = partial_sum
    highest, totals, running = (new_high, totals, running)
    context = (
        (running / jnp.transpose(totals)[:, :, None])
        .reshape(row_count, feature_count)
        .astype(jnp.bfloat16)
    )
    attended = frames + jnp.dot(context, output_weight, preferred_element_type=jnp.float32)
    mixer_in = norm_rows(attended, mixer_gain)
    half_width = KERNEL // 2
    padded = with_halo(mixer_in, (("ctx", 0),), half_width)
    convolved = jnp.zeros_like(mixer_in) + mixer_bias
    for tap_index in range(KERNEL):
        convolved = convolved + padded[tap_index : tap_index + row_count] * depthwise[tap_index]
    return attended + jax.nn.silu(convolved)


def solution(mesh):
    in_specs = (P(("session", "ctx"), None), P(), P(), P(), P(), P(), P(), P(), P())
    out_specs = P(("session", "ctx"), None)
    return jax.shard_map(
        per_device, mesh=mesh, in_specs=in_specs, out_specs=out_specs, check_vma=False
    )
```

profile of v0, /device:TPU:16, one launch (start us, length us, event | category | flops | bytes accessed | tf_op | source)
XLA Modules:
  0.0 314.0 jit_solution(9778761787293347411)
XLA Ops:
  6.5 0.0 copy-start
  6.5 0.0 copy-start.2
  6.5 0.0 all-gather.5.cloned.1.call-start
  6.5 1.4 reduce_sum.45
  8.0 1.4 multiply_reduce_fusion.2
  9.3 3.3 %convolution_convert_fusion = bf16[192,1024]{1,0:T(8,128)(2,1)} fusion(bf16[1024,1024]{1,0:T(8,128)(2,1)} %param.12, f32[192,1024]{1,0:T(8,128)} %param.9, f32[1024]{0:T(1024)} %param.10, f32[192]{0:T(256)S(1)} %add_rsqrt_fusion.1, f32[192]{0:T(256)S(1)} %broadcast_multiply_fusion.1), kind=kOutput, calls=%fused_computation.37 | convolution fusion | flops 403636224 | bytes 3282432 | tf_op jit(solution)/shard_map/dot_general | solution.py:30
  12.6 0.0 all-gather.5.cloned.1.call-update
  12.6 0.0 all-gather.3.cloned.1.call-start
  12.7 3.2 %convolution_convert_fusion.2 = bf16[192,1024]{1,0:T(8,128)(2,1)} fusion(bf16[1024,1024]{1,0:T(8,128)(2,1)} %param.13, f32[192,1024]{1,0:T(8,128)} %param.9, f32[1024]{0:T(1024)} %param.10, f32[192]{0:T(256)S(1)} %add_rsqrt_fusion.1, f32[192]{0:T(256)S(1)} %broadcast_multiply_fusion.1), kind=kOutput, calls=%fused_computation.39 | convolution fusion | flops 403636224 | bytes 3282432 | tf_op jit(solution)/shard_map/dot_general | solution.py:30
  15.9 0.0 all-gather.3.cloned.1.call-update
  15.9 2.5 convolution_convert_fusion.1
  18.4 0.2 copy.14
  18.6 0.0 copy-done.2
  18.6 0.1 fusion.106
  18.7 113.9 %all-gather.5.cloned.1.call-done = bf16[6144,1024]{1,0:T(8,128)(2,1)} async-done(((bf16[192,1024]{1,0:T(8,128)(2,1)}), bf16[6144,1024]{1,0:T(8,128)(2,1)}) %all-gather.5.cloned.1.call-update) | async-done | bytes 12582928 | tf_op jit(solution)/shard_map/all_gather | solution.py:51
  132.7 16.7 %copy.15 = bf16[6144,1024]{0,1:T(8,128)(2,1)} copy(bf16[6144,1024]{1,0:T(8,128)(2,1)} %all-gather.5.cloned.1.call-done) | data formatting | bytes 25165824 | tf_op jit(solution)/shard_map/all_gather | solution.py:51
  149.4 30.4 %multiply_reduce_fusion = (f32[16,192]{1,0:T(8,128)S(1)}, f32[16,192,6144]{2,1,0:T(8,128)}) fusion(bf16[192,16,64]{0,2,1:T(8,128)(2,1)S(1)} %bitcast.53, bf16[6144,16,64]{0,2,1:T(8,128)(2,1)} %bitcast.50), kind=kOutput, calls=%fused_computation.1 | convolution fusion | flops 2453664768 | bytes 88485888 | tf_op jit(solution)/shard_map/qhd,khd->hqk/dot_general | solution.py:59
  179.8 25.1 %fusion = f32[16,192]{1,0:T(8,128)S(1)} fusion(f32[16,192,6144]{2,1,0:T(8,128)} %get-tuple-element.39, f32[16,192]{1,0:T(8,128)S(1)} %broadcast_maximum_fusion), kind=kLoop, calls=%fused_computation.2 | loop fusion | flops 56620032 | bytes 75522048 | tf_op jit(solution)/shard_map/reduce_sum | solution.py:70
  204.9 44.5 %all-gather.3.cloned.1.call-done = bf16[6144,1024]{1,0:T(8,128)(2,1)} async-done(((bf16[192,1024]{1,0:T(8,128)(2,1)}), bf16[6144,1024]{1,0:T(8,128)(2,1)}) %all-gather.3.cloned.1.call-update) | async-done | bytes 12582928 | tf_op jit(solution)/shard_map/all_gather | solution.py:55
  249.4 16.7 %copy.13 = bf16[6144,1024]{0,1:T(8,128)(2,1)} copy(bf16[6144,1024]{1,0:T(8,128)(2,1)} %all-gather.3.cloned.1.call-done) | data formatting | bytes 25165824 | tf_op jit(solution)/shard_map/all_gather | solution.py:55
  266.1 0.0 copy-start.1
  266.1 0.0 copy-start.3
  266.1 0.0 copy-start.4
  266.1 29.8 %fusion.12 = bf16[192,16,64]{0,2,1:T(8,128)(2,1)S(1)} fusion(bf16[6144,16,64]{0,2,1:T(8,128)(2,1)} %bitcast.51, f32[16,192,6144]{2,1,0:T(8,128)} %get-tuple-element.39, f32[16,192]{1,0:T(8,128)S(1)} %broadcast_maximum_fusion, f32[192,16]{0,1:T(8,128)S(1)} %bitcast.54), kind=kOutput, calls=%fused_computation.41 | convolution fusion | flops 2472935424 | bytes 88498176 | tf_op jit(solution)/shard_map/hqk,khd->qhd/dot_general | solution.py:64
  295.9 0.0 copy-done
  295.9 0.0 copy-done.1
  296.0 0.7 fusion.108
  296.7 0.2 multiply_reduce_fusion.1
  296.9 0.0 copy-done.3
  296.9 0.2 multiply_multiply_fusion
  297.1 2.2 collective-permute-start
  299.3 1.3 collective-permute-start.1
  300.6 1.1 fusion.107
  301.7 0.0 collective-permute-done
  301.7 1.0 collective-permute-done.1
  302.7 0.0 copy-done.4
  302.7 4.4 %multiply_add_fusion = f32[192,1024]{1,0:T(8,128)} fusion(f32[192,1024]{1,0:T(8,128)S(1)} %get-tuple-element.41, f32[15,1024]{1,0:T(8,128)S(1)} %collective-permute-done.1, f32[192,1024]{1,0:T(8,128)S(1)} %multiply_multiply_fusion, f32[15,1024]{1,0:T(8,128)S(1)} %collective-permute-done, f32[1024]{0:T(1024)S(1)} %bitcast.84, f32[1024]{0:T(1024)S(1)} %bitcast.85, ...), kind=kLoop, calls=%fused_computation.157 | loop fusion | flops 19070976 | bytes 2613248 | tf_op jit(solution)/shard_map/add | solution.py:85
  (6 shorter events, 0.0 us)
Async XLA Ops:
  6.5 289.4 %copy-start = (bf16[1024,1024]{1,0:T(8,128)(2,1)S(1)}, bf16[1024,1024]{1,0:T(8,128)(2,1)}, u32[]{:S(2)}) copy-start(bf16[1024,1024]{1,0:T(8,128)(2,1)} %param.14) | copy-start | bytes 6291460
  6.5 12.1 %copy-start.2 = (f32[31,1024]{1,0:T(8,128)S(1)}, f32[31,1024]{1,0:T(8,128)}, u32[]{:S(2)}) copy-start(f32[31,1024]{1,0:T(8,128)} %param.16) | copy-start | bytes 380932
  6.5 126.1 %all-gather.5.cloned.1.call-start = ((), (), s32[]{:S(2)}) async-start(), calls=%async_computation.1 | async-start | bytes 12976128 | tf_op jit(solution)/shard_map/all_gather | solution.py:51
  12.6 236.8 %all-gather.3.cloned.1.call-start = ((), (), s32[]{:S(2)}) async-start(), calls=%async_computation | async-start | bytes 12976128 | tf_op jit(solution)/shard_map/all_gather | solution.py:55
  266.1 29.8 %copy-start.1 = (f32[192,1024]{1,0:T(8,128)S(1)}, f32[192,1024]{1,0:T(8,128)}, u32[]{:S(2)}) copy-start(f32[192,1024]{1,0:T(8,128)} %param.9) | copy-start | bytes 2359300
  266.1 30.8 %copy-start.3 = (f32[1024]{0:T(1024)S(1)}, f32[1024]{0:T(1024)}, u32[]{:S(2)}) copy-start(f32[1024]{0:T(1024)} %param.15) | copy-start | bytes 12292
  266.1 36.6 %copy-start.4 = (f32[1024]{0:T(1024)S(1)}, f32[1024]{0:T(1024)}, u32[]{:S(2)}) copy-start(f32[1024]{0:T(1024)} %param.17) | copy-start | bytes 12292
  297.1 4.6 %collective-permute-start = (f32[15,1024]{1,0:T(8,128)S(1)}, f32[15,1024]{1,0:T(8,128)S(1)}, u32[]{:S(2)}, u32[]{:S(2)}) collective-permute-start(f32[15,1024]{1,0:T(8,128)S(1)} %get-tuple-element.5), channel_id=1, source_target_pairs={{0,1},{1,2},{2,3},{3,4},{4,5},{5,6},{6,7},{7,8},{8,9},{9,10},{10,1... | collective-permute-start | bytes 184328 | tf_op jit(solution)/shard_map/ppermute | solution.py:15
  299.3 3.4 %collective-permute-start.1 = (f32[15,1024]{1,0:T(8,128)S(1)}, f32[15,1024]{1,0:T(8,128)S(1)}, u32[]{:S(2)}, u32[]{:S(2)}) collective-permute-start(f32[15,1024]{1,0:T(8,128)S(1)} %get-tuple-element.6), channel_id=1, source_target_pairs={{1,0},{2,1},{3,2},{4,3},{5,4},{6,5},{7,6},{8,7},{9,8},{10,9},{11,1... | collective-permute-start | bytes 184328 | tf_op jit(solution)/shard_map/ppermute | solution.py:18
Sparse Core Ops, SparseCore 0:
  12.7 119.8 all-gather.4
  135.4 113.9 all-gather.2
where the time goes:
time: 319 us; the launch traced here: 314 us
  waiting for transfers between devices  159 us (50%)
  matrix products  69.9 us (22%)
  local copies, waits for them, and re-layouts  34.9 us (11%)
  other arithmetic  32.7 us (10%)
  between operations  13.5 us (4%)
  starting transfers between devices  3.5 us (1%)
    all_gather x1, waiting for transfers between devices, per_device(): key_block = lax.all_gather(key_rows, 'ctx', axis=0, tiled=True)  114 us
    all_gather x1, waiting for transfers between devices, per_device(): lax.all_gather(value_rows, 'ctx', axis=0, tiled=True)  44.5 us
    dot_general x1, matrix products, per_device(): jnp.einsum('qhd,khd->hqk', query_heads, key_heads, preferred_element_type...  30.4 us
    dot_general x1, matrix products, per_device(): jnp.einsum('hqk,khd->qhd', weights.astype(jnp.bfloat16), value_heads, pre...  29.8 us
    reduce_sum x1, other arithmetic, per_device(): totals = jnp.sum(weights, axis=2)  25.1 us
    all_gather x1, local copies, waits for them, and re-layouts, per_device(): key_block = lax.all_gather(key_rows, 'ctx', axis=0, tiled=True)  16.7 us
    all_gather x1, local copies, waits for them, and re-layouts, per_device(): lax.all_gather(value_rows, 'ctx', axis=0, tiled=True)  16.7 us
    dot_general x3, matrix products, project(): jnp.dot(source, weight, preferred_element_type=jnp.float32)  8.98 us
  transfers between devices with their start and end apart: 4, of which 3 were waited for; matrix products, arithmetic and copies ran while one was open for 25% of the time, Pallas kernels for 0%

commit v1 on v0

v1 whole, which is shorter than its diff:
```python
import functools
import math

import jax
import jax.numpy as jnp
from jax import lax
from jax.experimental import pallas as pl
from jax.experimental.pallas import tpu as pltpu
from jax.sharding import PartitionSpec as P

F32, BF16 = jnp.float32, jnp.bfloat16
MESH = pl.DeviceIdType.MESH
HEADS = 16
HEAD = 64
KERNEL = 31
ROWS = 192
HALF = ROWS // 2
D = 1024
CHIPS = 16
EDGE = 16
BQ = 4 * ROWS
BK = 8 * ROWS
SCALE = HEAD**-0.5 * math.log2(math.e)
OFFSETS = (
    (0, 0), (0, 1), (0, 7), (1, 0),
    (0, 2), (0, 6), (1, 1), (1, 7),
    (0, 3), (0, 5), (1, 2), (1, 6),
    (0, 4), (1, 3), (1, 5), (1, 4),
)


def rows_at(index, size):
    return pl.ds(pl.multiple_of(index * size, size), size)


def norm(values, gain):
    center = jnp.mean(values, axis=1, keepdims=True)
    spread = jnp.mean(jnp.square(values - center), axis=1, keepdims=True)
    return (values - center) * lax.rsqrt(spread + 1e-05) * gain


def low_lanes(shape):
    return lax.broadcasted_iota(jnp.int32, shape, 1) < HEAD


def swap(values):
    return pltpu.roll(values, HEAD, 1)


def kernel(
    frames_hbm, again_ref, wq_hbm, wk_hbm, wv_hbm, wo_hbm, mgain_ref, taps_ref, bias_ref,
    out_ref,
    frames, wq, wk, wv, wo, normed,
    sendq, sendkv, qbuf, kvbuf, qx, vx, m_ref, o_ref, sendc, cbuf, context, attended, padded,
    load_sem, own_sem, q_send, q_recv, kv_send, kv_recv, f_send, f_recv, c_send, c_recv, h_send, h_recv,
):
    ctx = lax.axis_index("ctx")
    core = lax.rem(ctx, 2)
    chip = ctx // 2
    z, xh = lax.rem(chip, 8), chip // 8
    partner = chip * 2 + 1 - core

    def toward(r):
        dx, dz = OFFSETS[r]
        return lax.rem(xh + dx, 2) * 8 + lax.rem(z + dz, 8)

    def behind(r):
        dx, dz = OFFSETS[r]
        return lax.rem(xh + dx, 2) * 8 + lax.rem(z + 8 - dz, 8)

    def remote(src, dst, send, recv, target):
        return pltpu.make_async_remote_copy(
            src_ref=src, dst_ref=dst, send_sem=send, recv_sem=recv, device_id={"ctx": target}, device_id_type=MESH
        )

    loads = [
        pltpu.make_async_copy(src, dst, load_sem.at[n])
        for n, (src, dst) in enumerate(
            ((frames_hbm, frames), (wq_hbm, wq), (wk_hbm, wk), (wv_hbm, wv), (wo_hbm, wo))
        )
    ]
    for load in loads:
        load.start()

    barrier = pltpu.get_barrier_semaphore()
    greeted = [toward(r) * 2 + core for r in range(1, CHIPS)]
    greeted += [partner, lax.rem(ctx + 31 + 2 * core, 32)]
    for device in greeted:
        pl.semaphore_signal(barrier, inc=1, device_id={"ctx": device}, device_id_type=MESH)

    loads[0].wait()
    normed[...] = norm(frames[...], again_ref[...]).astype(BF16)
    low = low_lanes((ROWS, 128))
    low_half = low_lanes((HALF, 128))
    loads[1].wait()

    def project_q(g, carry):
        cols = rows_at(g, 256)
        q = jnp.dot(normed[...], wq[:, cols], preferred_element_type=F32)
        for pair in range(2):
            piece = q[:, pair * 128 : pair * 128 + 128]
            top, bottom = piece[:HALF], piece[HALF:]
            sendq[4 * g + 2 * pair] = jnp.where(low_half, top, swap(bottom)).astype(BF16)
            sendq[4 * g + 2 * pair + 1] = jnp.where(low_half, swap(top), bottom).astype(BF16)
        return carry

    lax.fori_loop(0, 4, project_q, 0)
    loads[2].wait()
    loads[3].wait()

    def project_kv(g, carry):
        cols = rows_at(g, 256)
        k = jnp.dot(normed[...], wk[:, cols], preferred_element_type=F32)
        v = jnp.dot(normed[...], wv[:, cols], preferred_element_type=F32)
        for pair in range(2):
            kp, vp = k[:, pair * 128 : pair * 128 + 128], v[:, pair * 128 : pair * 128 + 128]
            sendkv[4 * g + 2 * pair] = jnp.where(low, kp, swap(vp)).astype(BF16)
            sendkv[4 * g + 2 * pair + 1] = jnp.where(low, swap(kp), vp).astype(BF16)
        return carry

    lax.fori_loop(0, 4, project_kv, 0)

    def reset(n, carry):
        m_ref[rows_at(n, BQ), :] = jnp.full((BQ, 128), -jnp.inf, F32)
        o_ref[rows_at(n, BQ), :] = jnp.zeros((BQ, 128), F32)
        return carry

    lax.fori_loop(0, CHIPS * ROWS // BQ, reset, 0)
    pl.semaphore_wait(barrier, len(greeted))

    def q_copy(r):
        p = toward(r)
        return remote(sendq.at[p], qbuf.at[r], q_send.at[r], q_recv.at[r], p * 2 + core)

    def kv_rows(slot, which):
        return pl.ds(pl.multiple_of((slot * 2 + which) * ROWS, ROWS), ROWS)

    def kv_copy(r):
        p = toward(r)
        return remote(sendkv.at[p], kvbuf.at[kv_rows(r, core)], kv_send.at[r], kv_recv.at[r], p * 2 + core)

    own_q = pltpu.make_async_copy(sendq.at[chip], qbuf.at[0], own_sem.at[0])
    own_kv = pltpu.make_async_copy(sendkv.at[chip], kvbuf.at[kv_rows(0, core)], own_sem.at[1])
    own_forward = remote(sendkv.at[chip], kvbuf.at[kv_rows(0, core)], f_send.at[0], f_recv.at[0], partner)
    own_q.start()
    own_kv.start()
    own_forward.start()
    q_copies, kv_copies = [None] * CHIPS, [None] * CHIPS
    order = [("q", r) for r in range(1, 4)] + [("kv", r) for r in range(1, 4)]
    order += [("q", r) for r in range(4, CHIPS)] + [("kv", r) for r in range(4, CHIPS)]
    for kind, r in order:
        copy = q_copy(r) if kind == "q" else kv_copy(r)
        copy.start()
        (q_copies if kind == "q" else kv_copies)[r] = copy

    def q_arrival(slot):
        return remote(sendq.at[0], qbuf.at[slot], q_send.at[slot], q_recv.at[slot], partner)

    def kv_arrival(slot):
        return remote(sendkv.at[0], kvbuf.at[kv_rows(slot, core)], kv_send.at[slot], kv_recv.at[slot], partner)

    def forward(slot):
        mine = kvbuf.at[kv_rows(slot, core)]
        return remote(mine, mine, f_send.at[slot], f_recv.at[slot], partner)

    def forwarded(slot):
        theirs = kvbuf.at[kv_rows(slot, 1 - core)]
        return remote(theirs, theirs, f_send.at[slot], f_recv.at[slot], partner)

    own_q.wait()
    own_kv.wait()
    for r in range(1, 4):
        kv_arrival(r).wait_recv()
        forward(r).start()

    def unpack_q(slot):
        x = qbuf[slot].astype(F32)
        at = pl.multiple_of(slot * ROWS, ROWS)
        qx[pl.ds(at, HALF), :] = jnp.where(low_half, x, 0.0).astype(BF16)
        qx[pl.ds(at + HALF, HALF), :] = jnp.where(low_half, swap(x), 0.0).astype(BF16)

    low_wide = low_lanes((2 * ROWS, 128))

    def attend(t, carry):
        j, turn = t // 4, lax.rem(t, 4)
        i = jnp.where(j == 3, 3 - turn, turn)

        @pl.when(j == 0)
        def _():
            for s in range(4):
                @pl.when(i * 4 + s > 0)
                def _():
                    q_arrival(i * 4 + s).wait_recv()
                unpack_q(i * 4 + s)

        @pl.when(turn == 0)
        def _():
            for s in range(4):
                slot = j * 4 + s
                forwarded(slot).wait_recv()
                at = rows_at(slot, 2 * ROWS)
                x = kvbuf[at, :]
                vx[at, :] = jnp.where(low_wide, jnp.ones_like(x), x)

        @pl.when((turn == 3) & (j < 3))
        def _():
            for s in range(4):
                slot = j * 4 + 4 + s
                kv_arrival(slot).wait_recv()
                forward(slot).start()

        q = qx[rows_at(i, BQ), :]
        scores = lax.dot_general(
            q, kvbuf[rows_at(j, BK), :], (((1,), (1,)), ((), ())), preferred_element_type=F32
        )
        old = m_ref[rows_at(i, BQ), :]
        new = jnp.maximum(old, jnp.max(scores, axis=1, keepdims=True))
        weights = jnp.exp2((scores - jnp.concatenate([new] * (BK // 128), axis=1)) * SCALE).astype(BF16)
        part = jnp.dot(weights, vx[rows_at(j, BK), :], preferred_element_type=F32)
        o_ref[rows_at(i, BQ), :] = o_ref[rows_at(i, BQ), :] * jnp.exp2((old - new) * SCALE) + part
        m_ref[rows_at(i, BQ), :] = new

        @pl.when(j == 3)
        def _():
            for s in range(4):
                o = o_ref[rows_at(i * 4 + s, ROWS), :]
                c = o / swap(o)
                sendc[i * 4 + s] = jnp.where(low_half, swap(c[:HALF]), c[HALF:]).astype(BF16)
            for block in range(4):
                @pl.when(i == block)
                def _():
                    for r in range(block * 4, block * 4 + 4):
                        if r > 0:
                            remote(sendc.at[r], cbuf.at[chip], c_send.at[r], c_recv.at[r], behind(r) * 2 + core).start()

        return carry

    lax.fori_loop(0, 16, attend, 0)

    own_c = pltpu.make_async_copy(sendc.at[0], cbuf.at[chip], own_sem.at[2])
    own_c.start()
    loads[4].wait()
    own_c.wait()
    for r in range(1, CHIPS):
        remote(sendc.at[r], cbuf.at[toward(r)], c_send.at[r], c_recv.at[r], partner).wait_recv()
    for pair in range(HEADS // 2):
        a, b = cbuf[2 * pair].astype(F32), cbuf[2 * pair + 1].astype(F32)
        cols = slice(pair * 128, pair * 128 + 128)
        context[:HALF, cols] = jnp.where(low_half, a, swap(b)).astype(BF16)
        context[HALF:, cols] = jnp.where(low_half, swap(a), b).astype(BF16)
    attended[...] = frames[...] + jnp.dot(context[...], wo[...], preferred_element_type=F32)
    mixer_in = norm(attended[...], mgain_ref[...])
    for n in range(8):
        padded[n, EDGE : EDGE + ROWS, :] = mixer_in[:, n * 128 : n * 128 + 128]

    after, before = lax.rem(ctx + 1, 32), lax.rem(ctx + 31, 32)
    up = remote(
        padded.at[:, pl.ds(ROWS, EDGE)], padded.at[:, pl.ds(0, EDGE)], h_send.at[0], h_recv.at[0], after
    )
    down = remote(
        padded.at[:, pl.ds(EDGE, EDGE)], padded.at[:, pl.ds(EDGE + ROWS, EDGE)], h_send.at[1], h_recv.at[1], before
    )
    up.start()
    down.start()

    def convolve(first, count, above=None, below=None):
        def column(n, carry):
            lanes = rows_at(n, 128)
            weights = taps_ref[:, lanes]
            bias = bias_ref[:, lanes]
            for at in range(first, first + count, 8):
                total = jnp.broadcast_to(bias, (8, 128))
                for tap in range(KERNEL):
                    total = total + padded[n, at + tap + 1 : at + tap + 9, :] * weights[tap : tap + 1, :]
                out_ref[at : at + 8, lanes] = attended[at : at + 8, lanes] + total / (1.0 + jnp.exp(-total))
            return carry

        lax.fori_loop(0, 8, column, 0)

    convolve(EDGE, ROWS - 2 * EDGE)
    up.wait()
    down.wait()

    @pl.when(ctx == 0)
    def _():
        padded[:, :EDGE, :] = jnp.zeros((8, EDGE, 128), F32)

    @pl.when(ctx == 31)
    def _():
        padded[:, EDGE + ROWS :, :] = jnp.zeros((8, EDGE, 128), F32)

    convolve(0, EDGE)
    convolve(ROWS - EDGE, EDGE)

    own_forward.wait_send()
    for r in range(1, CHIPS):
        q_copies[r].wait_send()
        kv_copies[r].wait_send()
        forward(r).wait_send()
        remote(sendc.at[r], cbuf.at[chip], c_send.at[r], c_recv.at[r], partner).wait_send()


def per_device(frames, attend_gain, wq, wk, wv, wo, mixer_gain, depthwise, mixer_bias):
    hbm = pl.BlockSpec(memory_space=pl.ANY)
    vmem = pl.BlockSpec(memory_space=pltpu.VMEM)
    dma = pltpu.SemaphoreType.DMA
    return pl.pallas_call(
        kernel,
        out_shape=jax.ShapeDtypeStruct((ROWS, D), F32),
        in_specs=[hbm, vmem, hbm, hbm, hbm, hbm, vmem, vmem, vmem],
        out_specs=vmem,
        scratch_shapes=[
            pltpu.VMEM((ROWS, D), F32),
            *[pltpu.VMEM((D, D), BF16)] * 4,
            pltpu.VMEM((ROWS, D), BF16),
            pltpu.VMEM((HEADS, HALF, 128), BF16),
            pltpu.VMEM((HEADS, ROWS, 128), BF16),
            pltpu.VMEM((CHIPS, HALF, 128), BF16),
            pltpu.VMEM((CHIPS * 2 * ROWS, 128), BF16),
            pltpu.VMEM((CHIPS * ROWS, 128), BF16),
            pltpu.VMEM((CHIPS * 2 * ROWS, 128), BF16),
            pltpu.VMEM((CHIPS * ROWS, 128), F32),
            pltpu.VMEM((CHIPS * ROWS, 128), F32),
            pltpu.VMEM((CHIPS, HALF, 128), BF16),
            pltpu.VMEM((HEADS, HALF, 128), BF16),
            pltpu.VMEM((ROWS, D), BF16),
            pltpu.VMEM((ROWS, D), F32),
            pltpu.VMEM((8, ROWS + 2 * EDGE, 128), F32),
            dma((5,)), dma((3,)),
            *[dma((CHIPS,))] * 8,
            dma((2,)), dma((2,)),
        ],
        compiler_params=pltpu.CompilerParams(
            collective_id=0, has_side_effects=True, vmem_limit_bytes=60 * 1024 * 1024
        ),
        name="block",
    )(
        frames, attend_gain.reshape(1, D), wq, wk, wv, wo,
        mixer_gain.reshape(1, D), depthwise, mixer_bias.reshape(1, D),
    )


def solution(mesh):
    in_specs = (P(("session", "ctx"), None), P(), P(), P(), P(), P(), P(), P(), P())
    return jax.shard_map(
        per_device, mesh=mesh, in_specs=in_specs, out_specs=P(("session", "ctx"), None), check_vma=False
    )
```

time: 319 us -> 68.8 us (0.22); the launches traced: 314 us -> 68.7 us
  waiting for transfers between devices: 159 us -> 0 us
  matrix products: 69.9 us -> 0 us
  Pallas kernels: 0 us -> 66.6 us
  local copies, waits for them, and re-layouts: 34.9 us -> 2.09 us
  other arithmetic: 32.7 us -> 0 us
  between operations: 13.5 us -> 0.01 us
  starting transfers between devices: 3.5 us -> 0 us
    all_gather x2 -> x0, waiting for transfers between devices: 158 us -> none  [the longest x1 114 us: per_device(): key_block = lax.all_gather(key_rows, 'ctx', axis=0, tiled=True)]
    dot_general x6 -> x0, matrix products: 69.9 us -> none  [the longest x1 30.4 us: per_device(): jnp.einsum('qhd,khd->hqk', query_heads, key_heads, preferred_element_type...]
    pallas_call x0 -> x1, Pallas kernels: none -> 66.6 us  [per_device(): pl.pallas_call(kernel, out_shape=jax.ShapeDtypeStruct((ROWS, D), F32), in...]
    all_gather x2 -> x0, local copies, waits for them, and re-layouts: 33.4 us -> none  [the longest x1 16.7 us: per_device(): key_block = lax.all_gather(key_rows, 'ctx', axis=0, tiled=True)]
    reduce_sum x4 -> x0, other arithmetic: 28.1 us -> none  [the longest x1 25.1 us: per_device(): totals = jnp.sum(weights, axis=2)]
    add x1 -> x0, other arithmetic: 4.41 us -> none  [per_device(): return attended + jax.nn.silu(convolved)]
    ppermute x2 -> x0, starting transfers between devices: 3.46 us -> none  [the longest x1 2.17 us: with_halo(): lax.ppermute(lax.slice_in_dim(block, block.shape[dim] - width, None, axis...]
  transfers between devices with their start and end apart: 4 -> 0, of which waited for: 3 -> 0; matrix products, arithmetic and copies ran while one was open for 25% -> 0% of each run, Pallas kernels for 0% -> 0%
where the time goes in v1:
time: 68.8 us; the launch traced here: 68.7 us
  Pallas kernels  66.6 us (97%)
  local copies, waits for them, and re-layouts  2.09 us (3%)
    pallas_call x1, Pallas kernels, per_device(): pl.pallas_call(kernel, out_shape=jax.ShapeDtypeStruct((ROWS, D), F32), in...  66.6 us
    unnamed x1, local copies, waits for them, and re-layouts  2.09 us

profile of v1, /device:TPU:16, one launch (start us, length us, event | category | flops | bytes accessed | tf_op | source)
XLA Modules:
  0.0 68.7 jit_solution(17993108501897712367)
XLA Ops:
  0.0 66.6 %block.1 = f32[192,1024]{1,0:T(8,128)} custom-call(f32[192,1024]{1,0:T(8,128)} %frames_hbm.1, f32[1,1024]{1,0:T(1,128)} %bitcast.3, bf16[1024,1024]{1,0:T(8,128)(2,1)} %wq_hbm.1, bf16[1024,1024]{1,0:T(8,128)(2,1)} %wk_hbm.1, bf16[1024,1024]{1,0:T(8,128)(2,1)} %wv_hbm.1, bf16[1024,1024]{1,0:T(8,128)(2,1)} %wo_hbm.1, f32[1,1024]{1,0:T(1,128)} %bitcast.4, ...), custom_call_target="tpu_custom_call" | custom-call | tf_op jit(solution)/shard_map/block/pallas_call | solution.py:307
  66.6 2.1 %copy.11 = f32[192,1024]{1,0:T(8,128)} copy(f32[192,1024]{1,0:T(8,128)} %block.1) | data formatting | bytes 1572864

commit v2 on v1

v2 whole, which is shorter than its diff:
```python
import functools
import math

import jax
import jax.numpy as jnp
from jax import lax
from jax.experimental import pallas as pl
from jax.experimental.pallas import tpu as pltpu
from jax.sharding import PartitionSpec as P

F32, BF16 = jnp.float32, jnp.bfloat16
MESH = pl.DeviceIdType.MESH
HEADS = 16
HEAD = 64
KERNEL = 31
ROWS = 192
HALF = ROWS // 2
D = 1024
CHIPS = 16
EDGE = 16
BQ = 4 * ROWS
GRANT = 48 * 1024 * 1024
BK = 8 * ROWS
SCALE = HEAD**-0.5 * math.log2(math.e)
OFFSETS = (
    (0, 0), (0, 1), (0, 7), (1, 0),
    (0, 2), (0, 6), (1, 1), (1, 7),
    (0, 3), (0, 5), (1, 2), (1, 6),
    (0, 4), (1, 3), (1, 5), (1, 4),
)


def rows_at(index, size):
    return pl.ds(pl.multiple_of(index * size, size), size)


def norm(values, gain):
    center = jnp.mean(values, axis=1, keepdims=True)
    spread = jnp.mean(jnp.square(values - center), axis=1, keepdims=True)
    return (values - center) * lax.rsqrt(spread + 1e-05) * gain


def low_lanes(shape):
    return lax.broadcasted_iota(jnp.int32, shape, 1) < HEAD


def swap(values):
    return pltpu.roll(values, HEAD, 1)


def kernel(
    frames_hbm, again_hbm, wq_hbm, wk_hbm, wv_hbm, wo_hbm, mgain_hbm,
    padded, attended,
    frames, again_ref, wq, wk, wv, wo, mgain_ref, normed,
    sendq, sendkv, qbuf, kvbuf, qx, vx, m_ref, o_ref, sendc, cbuf, context, edges, halos,
    load_sem, own_sem, q_send, q_recv, kv_send, kv_recv, f_send, f_recv, c_send, c_recv, h_send, h_recv,
):
    ctx = lax.axis_index("ctx")
    core = lax.rem(ctx, 2)
    chip = ctx // 2
    z, xh = lax.rem(chip, 8), chip // 8
    partner = chip * 2 + 1 - core

    def toward(r):
        dx, dz = OFFSETS[r]
        return lax.rem(xh + dx, 2) * 8 + lax.rem(z + dz, 8)

    def behind(r):
        dx, dz = OFFSETS[r]
        return lax.rem(xh + dx, 2) * 8 + lax.rem(z + 8 - dz, 8)

    def remote(src, dst, send, recv, target):
        return pltpu.make_async_remote_copy(
            src_ref=src, dst_ref=dst, send_sem=send, recv_sem=recv, device_id={"ctx": target}, device_id_type=MESH
        )
    loads = [
        pltpu.make_async_copy(src, dst, load_sem.at[n])
        for n, (src, dst) in enumerate(
            (
                (frames_hbm, frames), (again_hbm, again_ref), (wq_hbm, wq), (wk_hbm, wk),
                (wv_hbm, wv), (wo_hbm, wo), (mgain_hbm, mgain_ref),
            )
        )
    ]
    for load in loads:
        load.start()

    barrier = pltpu.get_barrier_semaphore()
    greeted = [toward(r) * 2 + core for r in range(1, CHIPS)]
    greeted += [partner, lax.rem(ctx + 31 + 2 * core, 32)]
    for device in greeted:
        pl.semaphore_signal(barrier, inc=1, device_id={"ctx": device}, device_id_type=MESH)

    loads[0].wait()
    loads[1].wait()
    normed[...] = norm(frames[...], again_ref[...]).astype(BF16)
    low = low_lanes((ROWS, 128))
    low_half = low_lanes((HALF, 128))
    loads[2].wait()
    for g in range(4):
        q = jnp.dot(normed[...], wq[:, g * 256 : g * 256 + 256], preferred_element_type=F32)
        for pair in range(2):
            piece = q[:, pair * 128 : pair * 128 + 128]
            top, bottom = piece[:HALF], piece[HALF:]
            sendq[4 * g + 2 * pair] = jnp.where(low_half, top, swap(bottom)).astype(BF16)
            sendq[4 * g + 2 * pair + 1] = jnp.where(low_half, swap(top), bottom).astype(BF16)

    def q_copy(r):
        p = toward(r)
        return remote(sendq.at[p], qbuf.at[r], q_send.at[r], q_recv.at[r], p * 2 + core)

    def kv_rows(slot, which):
        return pl.ds(pl.multiple_of((slot * 2 + which) * ROWS, ROWS), ROWS)

    def kv_copy(r):
        p = toward(r)
        return remote(sendkv.at[p], kvbuf.at[kv_rows(r, core)], kv_send.at[r], kv_recv.at[r], p * 2 + core)

    q_copies, kv_copies = [None] * CHIPS, [None] * CHIPS

    def send(order):
        for kind, r in order:
            copy = q_copy(r) if kind == "q" else kv_copy(r)
            copy.start()
            (q_copies if kind == "q" else kv_copies)[r] = copy

    own_q = pltpu.make_async_copy(sendq.at[chip], qbuf.at[0], own_sem.at[0])
    own_q.start()
    pl.semaphore_wait(barrier, len(greeted))
    send([("q", r) for r in range(1, 8)])
    loads[3].wait()
    loads[4].wait()
    for g in range(4):
        k = jnp.dot(normed[...], wk[:, g * 256 : g * 256 + 256], preferred_element_type=F32)
        v = jnp.dot(normed[...], wv[:, g * 256 : g * 256 + 256], preferred_element_type=F32)
        for pair in range(2):
            kp, vp = k[:, pair * 128 : pair * 128 + 128], v[:, pair * 128 : pair * 128 + 128]
            sendkv[4 * g + 2 * pair] = jnp.where(low, kp, swap(vp)).astype(BF16)
            sendkv[4 * g + 2 * pair + 1] = jnp.where(low, swap(kp), vp).astype(BF16)
    own_kv = pltpu.make_async_copy(sendkv.at[chip], kvbuf.at[kv_rows(0, core)], own_sem.at[1])
    own_forward = remote(sendkv.at[chip], kvbuf.at[kv_rows(0, core)], f_send.at[0], f_recv.at[0], partner)
    own_kv.start()
    own_forward.start()
    send([("kv", r) for r in range(1, 4)] + [("q", r) for r in range(8, CHIPS)] + [("kv", r) for r in range(4, CHIPS)])

    def reset(n, carry):
        m_ref[rows_at(n, BQ), :] = jnp.full((BQ, 128), -jnp.inf, F32)
        o_ref[rows_at(n, BQ), :] = jnp.zeros((BQ, 128), F32)
        return carry

    lax.fori_loop(0, CHIPS * ROWS // BQ, reset, 0)
    def q_arrival(slot):
        return remote(sendq.at[0], qbuf.at[slot], q_send.at[slot], q_recv.at[slot], partner)

    def kv_arrival(slot):
        return remote(sendkv.at[0], kvbuf.at[kv_rows(slot, core)], kv_send.at[slot], kv_recv.at[slot], partner)

    def forward(slot):
        mine = kvbuf.at[kv_rows(slot, core)]
        return remote(mine, mine, f_send.at[slot], f_recv.at[slot], partner)

    def forwarded(slot):
        theirs = kvbuf.at[kv_rows(slot, 1 - core)]
        return remote(theirs, theirs, f_send.at[slot], f_recv.at[slot], partner)
    own_q.wait()
    own_kv.wait()
    for r in range(1, 4):
        kv_arrival(r).wait_recv()
        forward(r).start()

    def unpack_q(slot):
        x = qbuf[slot].astype(F32)
        at = pl.multiple_of(slot * ROWS, ROWS)
        qx[pl.ds(at, HALF), :] = jnp.where(low_half, x, 0.0).astype(BF16)
        qx[pl.ds(at + HALF, HALF), :] = jnp.where(low_half, swap(x), 0.0).astype(BF16)

    low_wide = low_lanes((2 * ROWS, 128))

    def attend(t, carry):
        j, turn = t // 4, lax.rem(t, 4)
        i = jnp.where(j == 3, 3 - turn, turn)
        @pl.when(j == 0)
        def _():
            for s in range(4):
                @pl.when(i * 4 + s > 0)
                def _():
                    q_arrival(i * 4 + s).wait_recv()
                unpack_q(i * 4 + s)
        @pl.when(turn == 0)
        def _():
            for s in range(4):
                slot = j * 4 + s
                forwarded(slot).wait_recv()
                at = rows_at(slot, 2 * ROWS)
                x = kvbuf[at, :]
                vx[at, :] = jnp.where(low_wide, jnp.ones_like(x), x)
        @pl.when((turn == 3) & (j < 3))
        def _():
            for s in range(4):
                slot = j * 4 + 4 + s
                kv_arrival(slot).wait_recv()
                forward(slot).start()
        q = qx[rows_at(i, BQ), :]
        scores = lax.dot_general(
            q, kvbuf[rows_at(j, BK), :], (((1,), (1,)), ((), ())), preferred_element_type=F32
        )
        old = m_ref[rows_at(i, BQ), :]
        new = jnp.maximum(old, jnp.max(scores, axis=1, keepdims=True))
        weights = jnp.exp2((scores - jnp.concatenate([new] * (BK // 128), axis=1)) * SCALE).astype(BF16)
        part = jnp.dot(weights, vx[rows_at(j, BK), :], preferred_element_type=F32)
        o_ref[rows_at(i, BQ), :] = o_ref[rows_at(i, BQ), :] * jnp.exp2((old - new) * SCALE) + part
        m_ref[rows_at(i, BQ), :] = new
        @pl.when(j == 3)
        def _():
            for s in range(4):
                o = o_ref[rows_at(i * 4 + s, ROWS), :]
                c = o / swap(o)
                sendc[i * 4 + s] = jnp.where(low_half, swap(c[:HALF]), c[HALF:]).astype(BF16)
            for block in range(4):
                @pl.when(i == block)
                def _():
                    for r in range(block * 4, block * 4 + 4):
                        if r > 0:
                            remote(sendc.at[r], cbuf.at[chip], c_send.at[r], c_recv.at[r], behind(r) * 2 + core).start()

        return carry
    lax.fori_loop(0, 16, attend, 0)

    own_c = pltpu.make_async_copy(sendc.at[0], cbuf.at[chip], own_sem.at[2])
    own_c.start()
    loads[5].wait()
    loads[6].wait()
    own_c.wait()
    for r in range(1, CHIPS):
        remote(sendc.at[r], cbuf.at[toward(r)], c_send.at[r], c_recv.at[r], partner).wait_recv()
    for pair in range(HEADS // 2):
        a, b = cbuf[2 * pair].astype(F32), cbuf[2 * pair + 1].astype(F32)
        cols = slice(pair * 128, pair * 128 + 128)
        context[:HALF, cols] = jnp.where(low_half, a, swap(b)).astype(BF16)
        context[HALF:, cols] = jnp.where(low_half, swap(a), b).astype(BF16)
    total = frames[...] + jnp.dot(context[...], wo[...], preferred_element_type=F32)
    mixer_in = norm(total, mgain_ref[...])
    for n in range(8):
        part = mixer_in[:, n * 128 : n * 128 + 128]
        edges[0, n] = part[:EDGE]
        edges[1, n] = part[ROWS - EDGE :]
        padded[n, EDGE : EDGE + ROWS, :] = part
        attended[n] = total[:, n * 128 : n * 128 + 128]

    after, before = lax.rem(ctx + 1, 32), lax.rem(ctx + 31, 32)
    up = remote(edges.at[1], halos.at[0], h_send.at[0], h_recv.at[0], after)
    down = remote(edges.at[0], halos.at[1], h_send.at[1], h_recv.at[1], before)
    up.start()
    down.start()
    up.wait()
    down.wait()
    padded[:, :EDGE, :] = jnp.where(ctx > 0, halos[0], 0.0)
    padded[:, EDGE + ROWS :, :] = jnp.where(ctx < 31, halos[1], 0.0)
    own_forward.wait_send()
    for r in range(1, CHIPS):
        q_copies[r].wait_send()
        kv_copies[r].wait_send()
        forward(r).wait_send()
        remote(sendc.at[r], cbuf.at[chip], c_send.at[r], c_recv.at[r], partner).wait_send()


def convolve(padded_ref, attended_ref, taps_ref, bias_ref, out_hbm, result, sems):
    def copy(n):
        return pltpu.make_async_copy(result.at[n], out_hbm.at[:, rows_at(n, 128)], sems.at[n])

    def column(n, carry):
        lanes = rows_at(n, 128)
        taps = taps_ref[:, lanes]
        bias = jnp.broadcast_to(bias_ref[:, lanes], (8, 128))
        for at in range(0, ROWS, 8):
            total = bias
            for tap in range(KERNEL):
                total = total + padded_ref[n, at + tap + 1 : at + tap + 9, :] * taps[tap : tap + 1, :]
            result[n, at : at + 8, :] = attended_ref[n, at : at + 8, :] + total / (1.0 + jnp.exp(-total))
        copy(n).start()
        return carry

    lax.fori_loop(0, 8, column, 0)
    for n in range(8):
        copy(n).wait()


def per_device(frames, attend_gain, wq, wk, wv, wo, mixer_gain, depthwise, mixer_bias):
    hbm = pl.BlockSpec(memory_space=pltpu.HBM)
    vmem = pl.BlockSpec(memory_space=pltpu.VMEM)
    dma = pltpu.SemaphoreType.DMA
    padded, attended = pl.pallas_call(
        kernel,
        out_shape=(
            jax.ShapeDtypeStruct((8, ROWS + 2 * EDGE, 128), F32),
            jax.ShapeDtypeStruct((8, ROWS, 128), F32),
        ),
        in_specs=[hbm] * 7,
        out_specs=(vmem, vmem),
        scratch_shapes=[
            pltpu.VMEM((ROWS, D), F32),
            pltpu.VMEM((1, D), F32),
            *[pltpu.VMEM((D, D), BF16)] * 4,
            pltpu.VMEM((1, D), F32),
            pltpu.VMEM((ROWS, D), BF16),
            pltpu.VMEM((HEADS, HALF, 128), BF16),
            pltpu.VMEM((HEADS, ROWS, 128), BF16),
            pltpu.VMEM((CHIPS, HALF, 128), BF16),
            pltpu.VMEM((CHIPS * 2 * ROWS, 128), BF16),
            pltpu.VMEM((CHIPS * ROWS, 128), BF16),
            pltpu.VMEM((CHIPS * 2 * ROWS, 128), BF16),
            pltpu.VMEM((CHIPS * ROWS, 128), F32),
            pltpu.VMEM((CHIPS * ROWS, 128), F32),
            pltpu.VMEM((CHIPS, HALF, 128), BF16),
            pltpu.VMEM((HEADS, HALF, 128), BF16),
            pltpu.VMEM((ROWS, D), BF16),
            pltpu.VMEM((2, 8, EDGE, 128), F32),
            pltpu.VMEM((2, 8, EDGE, 128), F32),
            dma((7,)), dma((3,)),
            *[dma((CHIPS,))] * 8,
            dma((2,)), dma((2,)),
        ],
        compiler_params=pltpu.CompilerParams(
            collective_id=0, has_side_effects=True, vmem_limit_bytes=GRANT
        ),
        name="block",
    )(*(pltpu.with_memory_space_constraint(a, pltpu.HBM) for a in (frames, attend_gain.reshape(1, D), wq, wk, wv, wo, mixer_gain.reshape(1, D))))
    return pl.pallas_call(
        convolve,
        out_shape=jax.ShapeDtypeStruct((ROWS, D), F32),
        in_specs=[vmem] * 4,
        out_specs=hbm,
        scratch_shapes=[pltpu.VMEM((8, ROWS, 128), F32), dma((8,))],
        compiler_params=pltpu.CompilerParams(vmem_limit_bytes=16 * 1024 * 1024),
        name="convolve",
    )(padded, attended, depthwise, mixer_bias.reshape(1, D))


def solution(mesh):
    in_specs = (P(("session", "ctx"), None), P(), P(), P(), P(), P(), P(), P(), P())
    return jax.shard_map(
        per_device, mesh=mesh, in_specs=in_specs, out_specs=P(("session", "ctx"), None), check_vma=False
    )
```

time: 68.8 us -> 65.1 us (0.946)
  local copies, waits for them, and re-layouts: 2.09 us -> 0.01 us
  Pallas kernels: 66.6 us -> 64.8 us
    unnamed x1 -> x4, local copies, waits for them, and re-layouts: 2.09 us -> 0.01 us
    pallas_call x1 -> x2, Pallas kernels: 66.6 us -> 64.8 us  [the longest x1 62 us: per_device(): pl.pallas_call(kernel, out_shape=(jax.ShapeDtypeStruct((8, ROWS + 2 * EDG...]
where the time goes in v2:
time: 65.1 us; the launch traced here: 64.8 us
  Pallas kernels  64.8 us (100%)
    pallas_call x1, Pallas kernels, per_device(): pl.pallas_call(kernel, out_shape=(jax.ShapeDtypeStruct((8, ROWS + 2 * EDG...  62 us
    pallas_call x1, Pallas kernels, per_device(): pl.pallas_call(convolve, out_shape=jax.ShapeDtypeStruct((ROWS, D), F32),...  2.79 us

profile of v2, /device:TPU:16, one launch (start us, length us, event | category | flops | bytes accessed | tf_op | source)
XLA Modules:
  0.0 64.8 jit_solution(14707476748820842179)
XLA Ops:
  0.0 0.0 copy-start
  0.0 0.0 copy-start.1
  0.0 62.0 %block.1 = (f32[8,224,128]{2,1,0:T(8,128)S(1)}, f32[8,192,128]{2,1,0:T(8,128)S(1)}) custom-call(f32[192,1024]{1,0:T(8,128)} %frames_hbm.1, f32[1,1024]{1,0:T(1,128)} %bitcast.4, bf16[1024,1024]{1,0:T(8,128)(2,1)} %wq_hbm.1, bf16[1024,1024]{1,0:T(8,128)(2,1)} %wk_hbm.1, bf16[1024,1024]{1,0:T(8,128)(2,1)} %wv_hbm.1, bf16[1024,1024]{1,0:T(8,128)(2,1)} %wo_hbm.1, ...), custom_call_target="tpu_custom_call" | custom-call | tf_op jit(solution)/shard_map/block/pallas_call | solution.py:292
  62.0 0.0 copy-done
  62.0 0.0 copy-done.1
  62.0 2.8 %convolve.1 = f32[192,1024]{1,0:T(8,128)} custom-call(f32[8,224,128]{2,1,0:T(8,128)S(1)} %get-tuple-element.7.padded_ref, f32[8,192,128]{2,1,0:T(8,128)S(1)} %get-tuple-element.8.attended_ref, f32[31,1024]{1,0:T(8,128)S(1)} %copy-done, f32[1,1024]{1,0:T(1,128)S(1)} %bitcast.3), custom_call_target="tpu_custom_call" | custom-call | tf_op jit(solution)/shard_map/convolve/pallas_call | solution.py:328
Async XLA Ops:
  0.0 62.0 %copy-start = (f32[31,1024]{1,0:T(8,128)S(1)}, f32[31,1024]{1,0:T(8,128)}, u32[]{:S(2)}) copy-start(f32[31,1024]{1,0:T(8,128)} %taps_ref.1) | copy-start | bytes 380932
  0.0 62.0 %copy-start.1 = (f32[1024]{0:T(1024)S(1)}, f32[1024]{0:T(1024)}, u32[]{:S(2)}) copy-start(f32[1024]{0:T(1024)} %param.17) | copy-start | bytes 12292

commit v3 on v2

--- a/solution.py
+++ b/solution.py
@@ -30,6 +30,23 @@
 )
 
 
+QUERY_BLOCKS = (0, 1, 0, 1, 2, 2, 3, 3, 3, 2, 3, 2, 1, 1, 0, 0)
+KEY_CHUNKS = (0, 0, 1, 1, 0, 1, 0, 1, 2, 2, 3, 3, 2, 3, 2, 3)
+
+
+def pick(step, table):
+    value = jnp.int32(table[0])
+    for n in range(1, len(table)):
+        if table[n] != table[0]:
+            value = jnp.where(step == n, table[n], value)
+    return value
+
+
+def first(step, table):
+    steps = [table.index(value) for value in range(4)]
+    return functools.reduce(jnp.logical_or, [step == n for n in steps])
+
+
 def rows_at(index, size):
     return pl.ds(pl.multiple_of(index * size, size), size)
 
@@ -48,11 +65,22 @@
     return pltpu.roll(values, HEAD, 1)
 
 
+def mix(n, starts, padded, attended, taps_ref, bias_ref, out, shift):
+    lanes = rows_at(n, 128)
+    taps = taps_ref[:, lanes]
+    bias = jnp.broadcast_to(bias_ref[:, lanes], (8, 128))
+    for at in starts:
+        total = bias
+        for tap in range(KERNEL):
+            total = total + padded[n, at + tap + 1 : at + tap + 9, :] * taps[tap : tap + 1, :]
+        out[n, at - shift : at - shift + 8, :] = attended[n, at : at + 8, :] + total / (1.0 + jnp.exp(-total))
+
+
 def kernel(
-    frames_hbm, again_hbm, wq_hbm, wk_hbm, wv_hbm, wo_hbm, mgain_hbm,
-    padded, attended,
+    frames_hbm, again_hbm, wq_hbm, wk_hbm, wv_hbm, wo_hbm, mgain_hbm, taps_hbm, bias_hbm,
+    padded, mixed,
     frames, again_ref, wq, wk, wv, wo, mgain_ref, normed,
-    sendq, sendkv, qbuf, kvbuf, qx, vx, m_ref, o_ref, sendc, cbuf, context, edges, halos,
+    sendq, sendkv, qbuf, kvbuf, qx, vx, m_ref, o_ref, sendc, cbuf, context, edges, halos, taps_ref, bias_ref,
     load_sem, own_sem, q_send, q_recv, kv_send, kv_recv, f_send, f_recv, c_send, c_recv, h_send, h_recv,
 ):
     ctx = lax.axis_index("ctx")
@@ -78,7 +106,7 @@
         for n, (src, dst) in enumerate(
             (
                 (frames_hbm, frames), (again_hbm, again_ref), (wq_hbm, wq), (wk_hbm, wk),
-                (wv_hbm, wv), (wo_hbm, wo), (mgain_hbm, mgain_ref),
+                (wv_hbm, wv), (wo_hbm, wo), (mgain_hbm, mgain_ref), (taps_hbm, taps_ref), (bias_hbm, bias_ref),
             )
         )
     ]
@@ -141,7 +169,7 @@
     own_forward = remote(sendkv.at[chip], kvbuf.at[kv_rows(0, core)], f_send.at[0], f_recv.at[0], partner)
     own_kv.start()
     own_forward.start()
-    send([("kv", r) for r in range(1, 4)] + [("q", r) for r in range(8, CHIPS)] + [("kv", r) for r in range(4, CHIPS)])
+    send([("kv", r) for r in range(1, 8)] + [("q", r) for r in range(8, CHIPS)] + [("kv", r) for r in range(8, CHIPS)])
 
     def reset(n, carry):
         m_ref[rows_at(n, BQ), :] = jnp.full((BQ, 128), -jnp.inf, F32)
@@ -177,16 +205,15 @@
     low_wide = low_lanes((2 * ROWS, 128))
 
     def attend(t, carry):
-        j, turn = t // 4, lax.rem(t, 4)
-        i = jnp.where(j == 3, 3 - turn, turn)
-        @pl.when(j == 0)
+        i, j = pick(t, QUERY_BLOCKS), pick(t, KEY_CHUNKS)
+        @pl.when(first(t, QUERY_BLOCKS))
         def _():
             for s in range(4):
                 @pl.when(i * 4 + s > 0)
                 def _():
                     q_arrival(i * 4 + s).wait_recv()
                 unpack_q(i * 4 + s)
-        @pl.when(turn == 0)
+        @pl.when(first(t, KEY_CHUNKS))
         def _():
             for s in range(4):
                 slot = j * 4 + s
@@ -194,10 +221,10 @@
                 at = rows_at(slot, 2 * ROWS)
                 x = kvbuf[at, :]
                 vx[at, :] = jnp.where(low_wide, jnp.ones_like(x), x)
-        @pl.when((turn == 3) & (j < 3))
+        @pl.when(first(t + 1, KEY_CHUNKS))
         def _():
             for s in range(4):
-                slot = j * 4 + 4 + s
+                slot = pick(t + 1, KEY_CHUNKS) * 4 + s
                 kv_arrival(slot).wait_recv()
                 forward(slot).start()
         q = qx[rows_at(i, BQ), :]
@@ -228,8 +255,8 @@
 
     own_c = pltpu.make_async_copy(sendc.at[0], cbuf.at[chip], own_sem.at[2])
     own_c.start()
-    loads[5].wait()
-    loads[6].wait()
+    for load in loads[5:]:
+        load.wait()
     own_c.wait()
     for r in range(1, CHIPS):
         remote(sendc.at[r], cbuf.at[toward(r)], c_send.at[r], c_recv.at[r], partner).wait_recv()
@@ -245,13 +272,19 @@
         edges[0, n] = part[:EDGE]
         edges[1, n] = part[ROWS - EDGE :]
         padded[n, EDGE : EDGE + ROWS, :] = part
-        attended[n] = total[:, n * 128 : n * 128 + 128]
+        mixed[n] = total[:, n * 128 : n * 128 + 128]
 
     after, before = lax.rem(ctx + 1, 32), lax.rem(ctx + 31, 32)
     up = remote(edges.at[1], halos.at[0], h_send.at[0], h_recv.at[0], after)
     down = remote(edges.at[0], halos.at[1], h_send.at[1], h_recv.at[1], before)
     up.start()
     down.start()
+
+    def interior(n, carry):
+        mix(n, range(EDGE, ROWS - EDGE, 8), padded, mixed, taps_ref, bias_ref, mixed, 0)
+        return carry
+
+    lax.fori_loop(0, 8, interior, 0)
     up.wait()
     down.wait()
     padded[:, :EDGE, :] = jnp.where(ctx > 0, halos[0], 0.0)
@@ -264,38 +297,44 @@
         remote(sendc.at[r], cbuf.at[chip], c_send.at[r], c_recv.at[r], partner).wait_send()
 
 
-def convolve(padded_ref, attended_ref, taps_ref, bias_ref, out_hbm, result, sems):
-    def copy(n):
-        return pltpu.make_async_copy(result.at[n], out_hbm.at[:, rows_at(n, 128)], sems.at[n])
+def convolve(padded_ref, mixed_ref, taps_ref, bias_ref, out_hbm, result, inner_sems, edge_sems):
+    def inner(n):
+        rows = pl.ds(EDGE, ROWS - 2 * EDGE)
+        return pltpu.make_async_copy(mixed_ref.at[n, rows], out_hbm.at[rows, rows_at(n, 128)], inner_sems.at[n])
+
+    def edge(n, side):
+        rows = pl.ds(side * (ROWS - EDGE), EDGE)
+        return pltpu.make_async_copy(result.at[n, side], out_hbm.at[rows, rows_at(n, 128)], edge_sems.at[n, side])
+
+    for n in range(8):
+        inner(n).start()
 
     def column(n, carry):
-        lanes = rows_at(n, 128)
-        taps = taps_ref[:, lanes]
-        bias = jnp.broadcast_to(bias_ref[:, lanes], (8, 128))
-        for at in range(0, ROWS, 8):
-            total = bias
-            for tap in range(KERNEL):
-                total = total + padded_ref[n, at + tap + 1 : at + tap + 9, :] * taps[tap : tap + 1, :]
-            result[n, at : at + 8, :] = attended_ref[n, at : at + 8, :] + total / (1.0 + jnp.exp(-total))
-        copy(n).start()
+        mix(n, range(0, EDGE, 8), padded_ref, mixed_ref, taps_ref, bias_ref, result.at[:, 0], 0)
+        mix(n, range(ROWS - EDGE, ROWS, 8), padded_ref, mixed_ref, taps_ref, bias_ref, result.at[:, 1], ROWS - EDGE)
+        edge(n, 0).start()
+        edge(n, 1).start()
         return carry
 
     lax.fori_loop(0, 8, column, 0)
     for n in range(8):
-        copy(n).wait()
+        inner(n).wait()
+        edge(n, 0).wait()
+        edge(n, 1).wait()
 
 
 def per_device(frames, attend_gain, wq, wk, wv, wo, mixer_gain, depthwise, mixer_bias):
     hbm = pl.BlockSpec(memory_space=pltpu.HBM)
     vmem = pl.BlockSpec(memory_space=pltpu.VMEM)
     dma = pltpu.SemaphoreType.DMA
-    padded, attended = pl.pallas_call(
+    bias = mixer_bias.reshape(1, D)
+    padded, mixed = pl.pallas_call(
         kernel,
         out_shape=(
             jax.ShapeDtypeStruct((8, ROWS + 2 * EDGE, 128), F32),
             jax.ShapeDtypeStruct((8, ROWS, 128), F32),
         ),
-        in_specs=[hbm] * 7,
+        in_specs=[hbm] * 9,
         out_specs=(vmem, vmem),
         scratch_shapes=[
             pltpu.VMEM((ROWS, D), F32),
@@ -316,7 +355,9 @@
             pltpu.VMEM((ROWS, D), BF16),
             pltpu.VMEM((2, 8, EDGE, 128), F32),
             pltpu.VMEM((2, 8, EDGE, 128), F32),
-            dma((7,)), dma((3,)),
+            pltpu.VMEM((KERNEL, D), F32),
+            pltpu.VMEM((1, D), F32),
+            dma((9,)), dma((3,)),
             *[dma((CHIPS,))] * 8,
             dma((2,)), dma((2,)),
         ],
@@ -324,16 +365,23 @@
             collective_id=0, has_side_effects=True, vmem_limit_bytes=GRANT
         ),
         name="block",
-    )(*(pltpu.with_memory_space_constraint(a, pltpu.HBM) for a in (frames, attend_gain.reshape(1, D), wq, wk, wv, wo, mixer_gain.reshape(1, D))))
+    )(
+        *(
+            pltpu.with_memory_space_constraint(value, pltpu.HBM)
+            for value in (
+                frames, attend_gain.reshape(1, D), wq, wk, wv, wo, mixer_gain.reshape(1, D), depthwise, bias,
+            )
+        )
+    )
     return pl.pallas_call(
         convolve,
         out_shape=jax.ShapeDtypeStruct((ROWS, D), F32),
         in_specs=[vmem] * 4,
         out_specs=hbm,
-        scratch_shapes=[pltpu.VMEM((8, ROWS, 128), F32), dma((8,))],
+        scratch_shapes=[pltpu.VMEM((8, 2, EDGE, 128), F32), dma((8,)), dma((8, 2))],
         compiler_params=pltpu.CompilerParams(vmem_limit_bytes=16 * 1024 * 1024),
         name="convolve",
-    )(padded, attended, depthwise, mixer_bias.reshape(1, D))
+    )(padded, mixed, depthwise, bias)
 
 
 def solution(mesh):

time: 65.1 us -> 62.7 us (0.963)
  Pallas kernels: 64.8 us -> 61.8 us
    pallas_call x1, Pallas kernels: 62 us -> 60.4 us  [per_device(): pl.pallas_call(kernel, out_shape=(jax.ShapeDtypeStruct((8, ROWS + 2 * EDG...]
    pallas_call x1, Pallas kernels: 2.79 us -> 1.37 us  [per_device(): pl.pallas_call(convolve, out_shape=jax.ShapeDtypeStruct((ROWS, D), F32),...]
where the time goes in v3:
time: 62.7 us; the launch traced here: 61.8 us
  Pallas kernels  61.8 us (99%)
    pallas_call x1, Pallas kernels, per_device(): pl.pallas_call(kernel, out_shape=(jax.ShapeDtypeStruct((8, ROWS + 2 * EDG...  60.4 us
    pallas_call x1, Pallas kernels, per_device(): pl.pallas_call(convolve, out_shape=jax.ShapeDtypeStruct((ROWS, D), F32),...  1.37 us

profile of v3, /device:TPU:16, one launch (start us, length us, event | category | flops | bytes accessed | tf_op | source)
XLA Modules:
  0.0 61.8 jit_solution(9795980997109105183)
XLA Ops:
  0.0 0.0 copy-start
  0.0 0.0 copy-start.1
  0.0 60.4 %block.1 = (f32[8,224,128]{2,1,0:T(8,128)S(1)}, f32[8,192,128]{2,1,0:T(8,128)S(1)}) custom-call(f32[192,1024]{1,0:T(8,128)} %frames_hbm.1, f32[1,1024]{1,0:T(1,128)} %bitcast.5, bf16[1024,1024]{1,0:T(8,128)(2,1)} %wq_hbm.1, bf16[1024,1024]{1,0:T(8,128)(2,1)} %wk_hbm.1, bf16[1024,1024]{1,0:T(8,128)(2,1)} %wv_hbm.1, bf16[1024,1024]{1,0:T(8,128)(2,1)} %wo_hbm.1, ...), custom_call_target="tpu_custom_call" | custom-call | tf_op jit(solution)/shard_map/block/pallas_call | solution.py:331
  60.4 0.0 copy-done
  60.4 0.0 copy-done.1
  60.4 1.4 %convolve.1 = f32[192,1024]{1,0:T(8,128)} custom-call(f32[8,224,128]{2,1,0:T(8,128)S(1)} %get-tuple-element.7.padded_ref, f32[8,192,128]{2,1,0:T(8,128)S(1)} %get-tuple-element.8.mixed_ref, f32[31,1024]{1,0:T(8,128)S(1)} %copy-done, f32[1,1024]{1,0:T(1,128)S(1)} %bitcast.4), custom_call_target="tpu_custom_call" | custom-call | tf_op jit(solution)/shard_map/convolve/pallas_call | solution.py:376
Async XLA Ops:
  0.0 60.4 %copy-start = (f32[31,1024]{1,0:T(8,128)S(1)}, f32[31,1024]{1,0:T(8,128)}, u32[]{:S(2)}) copy-start(f32[31,1024]{1,0:T(8,128)} %taps_ref.1) | copy-start | bytes 380932
  0.0 60.4 %copy-start.1 = (f32[1024]{0:T(1024)S(1)}, f32[1024]{0:T(1024)}, u32[]{:S(2)}) copy-start(f32[1024]{0:T(1024)} %param.17) | copy-start | bytes 12292

commit v4 on v3

--- a/solution.py
+++ b/solution.py
@@ -30,8 +30,10 @@
 )
 
 
-QUERY_BLOCKS = (0, 1, 0, 1, 2, 2, 3, 3, 3, 2, 3, 2, 1, 1, 0, 0)
-KEY_CHUNKS = (0, 0, 1, 1, 0, 1, 0, 1, 2, 2, 3, 3, 2, 3, 2, 3)
+STEPS = (
+    ((0, 0), (1, 0)), ((0, 1), (1, 1)), ((2, 0), (2, 1)), ((3, 0), (3, 1)),
+    ((3, 2), (2, 2)), ((3, 3), (2, 3)), ((1, 2), (1, 3)), ((0, 2), (0, 3)),
+)
 
 
 def pick(step, table):
@@ -40,11 +42,6 @@
         if table[n] != table[0]:
             value = jnp.where(step == n, table[n], value)
     return value
-
-
-def first(step, table):
-    steps = [table.index(value) for value in range(4)]
-    return functools.reduce(jnp.logical_or, [step == n for n in steps])
 
 
 def rows_at(index, size):
@@ -101,12 +98,15 @@
         return pltpu.make_async_remote_copy(
             src_ref=src, dst_ref=dst, send_sem=send, recv_sem=recv, device_id={"ctx": target}, device_id_type=MESH
         )
+    pieces = [slice(g * 256, g * 256 + 256) for g in range(4)]
     loads = [
         pltpu.make_async_copy(src, dst, load_sem.at[n])
         for n, (src, dst) in enumerate(
             (
-                (frames_hbm, frames), (again_hbm, again_ref), (wq_hbm, wq), (wk_hbm, wk),
-                (wv_hbm, wv), (wo_hbm, wo), (mgain_hbm, mgain_ref), (taps_hbm, taps_ref), (bias_hbm, bias_ref),
+                (frames_hbm, frames), (again_hbm, again_ref),
+                *[(wq_hbm.at[:, piece], wq.at[:, piece]) for piece in pieces],
+                (wk_hbm, wk), (wv_hbm, wv),
+                (wo_hbm, wo), (mgain_hbm, mgain_ref), (taps_hbm, taps_ref), (bias_hbm, bias_ref),
             )
         )
     ]
@@ -124,8 +124,8 @@
     normed[...] = norm(frames[...], again_ref[...]).astype(BF16)
     low = low_lanes((ROWS, 128))
     low_half = low_lanes((HALF, 128))
-    loads[2].wait()
     for g in range(4):
+        loads[2 + g].wait()
         q = jnp.dot(normed[...], wq[:, g * 256 : g * 256 + 256], preferred_element_type=F32)
         for pair in range(2):
             piece = q[:, pair * 128 : pair * 128 + 128]
@@ -154,10 +154,8 @@
 
     own_q = pltpu.make_async_copy(sendq.at[chip], qbuf.at[0], own_sem.at[0])
     own_q.start()
-    pl.semaphore_wait(barrier, len(greeted))
-    send([("q", r) for r in range(1, 8)])
-    loads[3].wait()
-    loads[4].wait()
+    loads[6].wait()
+    loads[7].wait()
     for g in range(4):
         k = jnp.dot(normed[...], wk[:, g * 256 : g * 256 + 256], preferred_element_type=F32)
         v = jnp.dot(normed[...], wv[:, g * 256 : g * 256 + 256], preferred_element_type=F32)
@@ -165,18 +163,20 @@
             kp, vp = k[:, pair * 128 : pair * 128 + 128], v[:, pair * 128 : pair * 128 + 128]
             sendkv[4 * g + 2 * pair] = jnp.where(low, kp, swap(vp)).astype(BF16)
             sendkv[4 * g + 2 * pair + 1] = jnp.where(low, swap(kp), vp).astype(BF16)
+    def reset(n, carry):
+        m_ref[rows_at(n, BQ), :] = jnp.full((BQ, 128), -jnp.inf, F32)
+        o_ref[rows_at(n, BQ), :] = jnp.zeros((BQ, 128), F32)
+        return carry
+
+    lax.fori_loop(0, CHIPS * ROWS // BQ, reset, 0)
+    pl.semaphore_wait(barrier, len(greeted))
+    send([("q", r) for r in range(1, 8)])
     own_kv = pltpu.make_async_copy(sendkv.at[chip], kvbuf.at[kv_rows(0, core)], own_sem.at[1])
     own_forward = remote(sendkv.at[chip], kvbuf.at[kv_rows(0, core)], f_send.at[0], f_recv.at[0], partner)
     own_kv.start()
     own_forward.start()
     send([("kv", r) for r in range(1, 8)] + [("q", r) for r in range(8, CHIPS)] + [("kv", r) for r in range(8, CHIPS)])
 
-    def reset(n, carry):
-        m_ref[rows_at(n, BQ), :] = jnp.full((BQ, 128), -jnp.inf, F32)
-        o_ref[rows_at(n, BQ), :] = jnp.zeros((BQ, 128), F32)
-        return carry
-
-    lax.fori_loop(0, CHIPS * ROWS // BQ, reset, 0)
     def q_arrival(slot):
         return remote(sendq.at[0], qbuf.at[slot], q_send.at[slot], q_recv.at[slot], partner)
 
@@ -196,37 +196,30 @@
         kv_arrival(r).wait_recv()
         forward(r).start()
 
-    def unpack_q(slot):
-        x = qbuf[slot].astype(F32)
-        at = pl.multiple_of(slot * ROWS, ROWS)
-        qx[pl.ds(at, HALF), :] = jnp.where(low_half, x, 0.0).astype(BF16)
-        qx[pl.ds(at + HALF, HALF), :] = jnp.where(low_half, swap(x), 0.0).astype(BF16)
-
-    low_wide = low_lanes((2 * ROWS, 128))
-
-    def attend(t, carry):
-        i, j = pick(t, QUERY_BLOCKS), pick(t, KEY_CHUNKS)
-        @pl.when(first(t, QUERY_BLOCKS))
-        def _():
-            for s in range(4):
-                @pl.when(i * 4 + s > 0)
-                def _():
-                    q_arrival(i * 4 + s).wait_recv()
-                unpack_q(i * 4 + s)
-        @pl.when(first(t, KEY_CHUNKS))
-        def _():
-            for s in range(4):
-                slot = j * 4 + s
-                forwarded(slot).wait_recv()
-                at = rows_at(slot, 2 * ROWS)
-                x = kvbuf[at, :]
-                vx[at, :] = jnp.where(low_wide, jnp.ones_like(x), x)
-        @pl.when(first(t + 1, KEY_CHUNKS))
-        def _():
-            for s in range(4):
-                slot = pick(t + 1, KEY_CHUNKS) * 4 + s
-                kv_arrival(slot).wait_recv()
-                forward(slot).start()
+    def unpack_q(block, skip=0):
+        for s in range(skip, 4):
+            q_arrival(block * 4 + s).wait_recv()
+        for s in range(4):
+            x = qbuf[block * 4 + s].astype(F32)
+            at = pl.multiple_of((block * 4 + s) * ROWS, ROWS)
+            qx[pl.ds(at, HALF), :] = jnp.where(low_half, x, 0.0).astype(BF16)
+            qx[pl.ds(at + HALF, HALF), :] = jnp.where(low_half, swap(x), 0.0).astype(BF16)
+
+    def pass_on(chunk):
+        for s in range(4):
+            kv_arrival(chunk * 4 + s).wait_recv()
+            forward(chunk * 4 + s).start()
+
+    low_wide = low_lanes((8 * ROWS, 128))
+
+    def open_chunk(chunk):
+        for s in range(4):
+            forwarded(chunk * 4 + s).wait_recv()
+        at = rows_at(chunk, BK)
+        x = kvbuf[at, :]
+        vx[at, :] = jnp.where(low_wide, jnp.ones_like(x), x)
+
+    def attend(i, j):
         q = qx[rows_at(i, BQ), :]
         scores = lax.dot_general(
             q, kvbuf[rows_at(j, BK), :], (((1,), (1,)), ((), ())), preferred_element_type=F32
@@ -237,25 +230,46 @@
         part = jnp.dot(weights, vx[rows_at(j, BK), :], preferred_element_type=F32)
         o_ref[rows_at(i, BQ), :] = o_ref[rows_at(i, BQ), :] * jnp.exp2((old - new) * SCALE) + part
         m_ref[rows_at(i, BQ), :] = new
-        @pl.when(j == 3)
-        def _():
-            for s in range(4):
-                o = o_ref[rows_at(i * 4 + s, ROWS), :]
-                c = o / swap(o)
-                sendc[i * 4 + s] = jnp.where(low_half, swap(c[:HALF]), c[HALF:]).astype(BF16)
-            for block in range(4):
-                @pl.when(i == block)
-                def _():
-                    for r in range(block * 4, block * 4 + 4):
-                        if r > 0:
-                            remote(sendc.at[r], cbuf.at[chip], c_send.at[r], c_recv.at[r], behind(r) * 2 + core).start()
+
+    def give_back(block):
+        for s in range(4):
+            o = o_ref[(block * 4 + s) * ROWS : (block * 4 + s + 1) * ROWS, :]
+            c = o / swap(o)
+            sendc[block * 4 + s] = jnp.where(low_half, swap(c[:HALF]), c[HALF:]).astype(BF16)
+        for r in range(block * 4, block * 4 + 4):
+            if r > 0:
+                remote(sendc.at[r], cbuf.at[chip], c_send.at[r], c_recv.at[r], behind(r) * 2 + core).start()
+    unpack_q(0, 1)
+    unpack_q(1)
+
+    def step(t, carry):
+        opened = {0: 0, 1: 1, 4: 2, 5: 3}
+        for when, chunk in opened.items():
+            @pl.when(t == when)
+            def _():
+                open_chunk(chunk)
+        for when, block in {2: 2, 3: 3}.items():
+            @pl.when(t == when)
+            def _():
+                unpack_q(block)
+        for half in range(2):
+            attend(pick(t, [pair[half][0] for pair in STEPS]), pick(t, [pair[half][1] for pair in STEPS]))
+        for when, chunk in {0: 1, 3: 2, 4: 3}.items():
+            @pl.when(t == when)
+            def _():
+                pass_on(chunk)
+        for when, blocks in {5: (3, 2), 6: (1,), 7: (0,)}.items():
+            @pl.when(t == when)
+            def _():
+                for block in blocks:
+                    give_back(block)
 
         return carry
-    lax.fori_loop(0, 16, attend, 0)
+    lax.fori_loop(0, len(STEPS), step, 0)
 
     own_c = pltpu.make_async_copy(sendc.at[0], cbuf.at[chip], own_sem.at[2])
     own_c.start()
-    for load in loads[5:]:
+    for load in loads[8:]:
         load.wait()
     own_c.wait()
     for r in range(1, CHIPS):
@@ -357,7 +371,7 @@
             pltpu.VMEM((2, 8, EDGE, 128), F32),
             pltpu.VMEM((KERNEL, D), F32),
             pltpu.VMEM((1, D), F32),
-            dma((9,)), dma((3,)),
+            dma((12,)), dma((3,)),
             *[dma((CHIPS,))] * 8,
             dma((2,)), dma((2,)),
         ],

time: 62.7 us -> 63.4 us (1.011); the launches traced: 61.8 us -> 63.4 us
  Pallas kernels: 61.8 us -> 63.3 us
    pallas_call x1, Pallas kernels: 60.4 us -> 62 us  [per_device(): pl.pallas_call(kernel, out_shape=(jax.ShapeDtypeStruct((8, ROWS + 2 * EDG...]
where the time goes in v4:
time: 63.4 us
  Pallas kernels  63.3 us (100%)
    pallas_call x1, Pallas kernels, per_device(): pl.pallas_call(kernel, out_shape=(jax.ShapeDtypeStruct((8, ROWS + 2 * EDG...  62 us
    pallas_call x1, Pallas kernels, per_device(): pl.pallas_call(convolve, out_shape=jax.ShapeDtypeStruct((ROWS, D), F32),...  1.37 us

profile of v4, /device:TPU:16, one launch (start us, length us, event | category | flops | bytes accessed | tf_op | source)
XLA Modules:
  0.0 63.4 jit_solution(8049061890283564743)
XLA Ops:
  0.0 0.0 copy-start
  0.0 0.0 copy-start.1
  0.0 62.0 %block.1 = (f32[8,224,128]{2,1,0:T(8,128)S(1)}, f32[8,192,128]{2,1,0:T(8,128)S(1)}) custom-call(f32[192,1024]{1,0:T(8,128)} %frames_hbm.1, f32[1,1024]{1,0:T(1,128)} %bitcast.5, bf16[1024,1024]{1,0:T(8,128)(2,1)} %wq_hbm.1, bf16[1024,1024]{1,0:T(8,128)(2,1)} %wk_hbm.1, bf16[1024,1024]{1,0:T(8,128)(2,1)} %wv_hbm.1, bf16[1024,1024]{1,0:T(8,128)(2,1)} %wo_hbm.1, ...), custom_call_target="tpu_custom_call" | custom-call | tf_op jit(solution)/shard_map/block/pallas_call | solution.py:345
  62.0 0.0 copy-done
  62.0 0.0 copy-done.1
  62.0 1.4 %convolve.1 = f32[192,1024]{1,0:T(8,128)} custom-call(f32[8,224,128]{2,1,0:T(8,128)S(1)} %get-tuple-element.7.padded_ref, f32[8,192,128]{2,1,0:T(8,128)S(1)} %get-tuple-element.8.mixed_ref, f32[31,1024]{1,0:T(8,128)S(1)} %copy-done, f32[1,1024]{1,0:T(1,128)S(1)} %bitcast.4), custom_call_target="tpu_custom_call" | custom-call | tf_op jit(solution)/shard_map/convolve/pallas_call | solution.py:390
Async XLA Ops:
  0.0 62.0 %copy-start = (f32[31,1024]{1,0:T(8,128)S(1)}, f32[31,1024]{1,0:T(8,128)}, u32[]{:S(2)}) copy-start(f32[31,1024]{1,0:T(8,128)} %taps_ref.1) | copy-start | bytes 380932
  0.0 62.0 %copy-start.1 = (f32[1024]{0:T(1024)S(1)}, f32[1024]{0:T(1024)}, u32[]{:S(2)}) copy-start(f32[1024]{0:T(1024)} %param.17) | copy-start | bytes 12292

commit v5 on v4

--- a/solution.py
+++ b/solution.py
@@ -30,10 +30,7 @@
 )
 
 
-STEPS = (
-    ((0, 0), (1, 0)), ((0, 1), (1, 1)), ((2, 0), (2, 1)), ((3, 0), (3, 1)),
-    ((3, 2), (2, 2)), ((3, 3), (2, 3)), ((1, 2), (1, 3)), ((0, 2), (0, 3)),
-)
+STEPS = (((0, 0), (1, 0)), ((0, 1), (1, 1)), ((2, 0), (2, 1)), ((3, 0), (3, 1)), ((3, 2), (2, 2)))
 
 
 def pick(step, table):
@@ -45,6 +42,8 @@
 
 
 def rows_at(index, size):
+    if isinstance(index, int):
+        return pl.ds(index * size, size)
     return pl.ds(pl.multiple_of(index * size, size), size)
 
 
@@ -98,19 +97,17 @@
         return pltpu.make_async_remote_copy(
             src_ref=src, dst_ref=dst, send_sem=send, recv_sem=recv, device_id={"ctx": target}, device_id_type=MESH
         )
-    pieces = [slice(g * 256, g * 256 + 256) for g in range(4)]
     loads = [
         pltpu.make_async_copy(src, dst, load_sem.at[n])
         for n, (src, dst) in enumerate(
             (
                 (frames_hbm, frames), (again_hbm, again_ref),
-                *[(wq_hbm.at[:, piece], wq.at[:, piece]) for piece in pieces],
-                (wk_hbm, wk), (wv_hbm, wv),
+                (wq_hbm, wq), (wk_hbm, wk), (wv_hbm, wv),
                 (wo_hbm, wo), (mgain_hbm, mgain_ref), (taps_hbm, taps_ref), (bias_hbm, bias_ref),
             )
         )
     ]
-    for load in loads:
+    for load in loads[:3]:
         load.start()
 
     barrier = pltpu.get_barrier_semaphore()
@@ -121,11 +118,13 @@
 
     loads[0].wait()
     loads[1].wait()
+    for load in loads[3:5]:
+        load.start()
     normed[...] = norm(frames[...], again_ref[...]).astype(BF16)
     low = low_lanes((ROWS, 128))
     low_half = low_lanes((HALF, 128))
+    loads[2].wait()
     for g in range(4):
-        loads[2 + g].wait()
         q = jnp.dot(normed[...], wq[:, g * 256 : g * 256 + 256], preferred_element_type=F32)
         for pair in range(2):
             piece = q[:, pair * 128 : pair * 128 + 128]
@@ -154,8 +153,12 @@
 
     own_q = pltpu.make_async_copy(sendq.at[chip], qbuf.at[0], own_sem.at[0])
     own_q.start()
-    loads[6].wait()
-    loads[7].wait()
+    pl.semaphore_wait(barrier, len(greeted))
+    send([("q", r) for r in range(1, 8)])
+    for load in loads[5:]:
+        load.start()
+    loads[3].wait()
+    loads[4].wait()
     for g in range(4):
         k = jnp.dot(normed[...], wk[:, g * 256 : g * 256 + 256], preferred_element_type=F32)
         v = jnp.dot(normed[...], wv[:, g * 256 : g * 256 + 256], preferred_element_type=F32)
@@ -163,14 +166,6 @@
             kp, vp = k[:, pair * 128 : pair * 128 + 128], v[:, pair * 128 : pair * 128 + 128]
             sendkv[4 * g + 2 * pair] = jnp.where(low, kp, swap(vp)).astype(BF16)
             sendkv[4 * g + 2 * pair + 1] = jnp.where(low, swap(kp), vp).astype(BF16)
-    def reset(n, carry):
-        m_ref[rows_at(n, BQ), :] = jnp.full((BQ, 128), -jnp.inf, F32)
-        o_ref[rows_at(n, BQ), :] = jnp.zeros((BQ, 128), F32)
-        return carry
-
-    lax.fori_loop(0, CHIPS * ROWS // BQ, reset, 0)
-    pl.semaphore_wait(barrier, len(greeted))
-    send([("q", r) for r in range(1, 8)])
     own_kv = pltpu.make_async_copy(sendkv.at[chip], kvbuf.at[kv_rows(0, core)], own_sem.at[1])
     own_forward = remote(sendkv.at[chip], kvbuf.at[kv_rows(0, core)], f_send.at[0], f_recv.at[0], partner)
     own_kv.start()
@@ -190,6 +185,13 @@
     def forwarded(slot):
         theirs = kvbuf.at[kv_rows(slot, 1 - core)]
         return remote(theirs, theirs, f_send.at[slot], f_recv.at[slot], partner)
+
+    def reset(n, carry):
+        m_ref[rows_at(n, BQ), :] = jnp.full((BQ, 128), -jnp.inf, F32)
+        o_ref[rows_at(n, BQ), :] = jnp.zeros((BQ, 128), F32)
+        return carry
+
+    lax.fori_loop(0, CHIPS * ROWS // BQ, reset, 0)
     own_q.wait()
     own_kv.wait()
     for r in range(1, 4):
@@ -243,7 +245,7 @@
     unpack_q(1)
 
     def step(t, carry):
-        opened = {0: 0, 1: 1, 4: 2, 5: 3}
+        opened = {0: 0, 1: 1, 4: 2}
         for when, chunk in opened.items():
             @pl.when(t == when)
             def _():
@@ -258,18 +260,24 @@
             @pl.when(t == when)
             def _():
                 pass_on(chunk)
-        for when, blocks in {5: (3, 2), 6: (1,), 7: (0,)}.items():
-            @pl.when(t == when)
-            def _():
-                for block in blocks:
-                    give_back(block)
 
         return carry
     lax.fori_loop(0, len(STEPS), step, 0)
+    attend(1, 2)
+    open_chunk(3)
+    attend(3, 3)
+    give_back(3)
+    attend(2, 3)
+    attend(1, 3)
+    give_back(2)
+    give_back(1)
+    attend(0, 2)
+    attend(0, 3)
+    give_back(0)
 
     own_c = pltpu.make_async_copy(sendc.at[0], cbuf.at[chip], own_sem.at[2])
     own_c.start()
-    for load in loads[8:]:
+    for load in loads[5:]:
         load.wait()
     own_c.wait()
     for r in range(1, CHIPS):
@@ -371,7 +379,7 @@
             pltpu.VMEM((2, 8, EDGE, 128), F32),
             pltpu.VMEM((KERNEL, D), F32),
             pltpu.VMEM((1, D), F32),
-            dma((12,)), dma((3,)),
+            dma((9,)), dma((3,)),
             *[dma((CHIPS,))] * 8,
             dma((2,)), dma((2,)),
         ],

time: 63.4 us -> 62.4 us (0.984)
  Pallas kernels: 63.3 us -> 61.6 us
    pallas_call x1, Pallas kernels: 62 us -> 60.2 us  [per_device(): pl.pallas_call(kernel, out_shape=(jax.ShapeDtypeStruct((8, ROWS + 2 * EDG...]
where the time goes in v5:
time: 62.4 us; the launch traced here: 61.8 us
  Pallas kernels  61.6 us (99%)
    pallas_call x1, Pallas kernels, per_device(): pl.pallas_call(kernel, out_shape=(jax.ShapeDtypeStruct((8, ROWS + 2 * EDG...  60.2 us
    pallas_call x1, Pallas kernels, per_device(): pl.pallas_call(convolve, out_shape=jax.ShapeDtypeStruct((ROWS, D), F32),...  1.37 us

profile of v5, /device:TPU:16, one launch (start us, length us, event | category | flops | bytes accessed | tf_op | source)
XLA Modules:
  0.0 61.8 jit_solution(5871037501342896382)
XLA Ops:
  0.0 0.0 copy-start
  0.0 0.0 copy-start.1
  0.0 60.2 %block.1 = (f32[8,224,128]{2,1,0:T(8,128)S(1)}, f32[8,192,128]{2,1,0:T(8,128)S(1)}) custom-call(f32[192,1024]{1,0:T(8,128)} %frames_hbm.1, f32[1,1024]{1,0:T(1,128)} %bitcast.5, bf16[1024,1024]{1,0:T(8,128)(2,1)} %wq_hbm.1, bf16[1024,1024]{1,0:T(8,128)(2,1)} %wk_hbm.1, bf16[1024,1024]{1,0:T(8,128)(2,1)} %wv_hbm.1, bf16[1024,1024]{1,0:T(8,128)(2,1)} %wo_hbm.1, ...), custom_call_target="tpu_custom_call" | custom-call | tf_op jit(solution)/shard_map/block/pallas_call | solution.py:353
  60.2 0.0 copy-done
  60.2 0.0 copy-done.1
  60.3 1.4 %convolve.1 = f32[192,1024]{1,0:T(8,128)} custom-call(f32[8,224,128]{2,1,0:T(8,128)S(1)} %get-tuple-element.7.padded_ref, f32[8,192,128]{2,1,0:T(8,128)S(1)} %get-tuple-element.8.mixed_ref, f32[31,1024]{1,0:T(8,128)S(1)} %copy-done, f32[1,1024]{1,0:T(1,128)S(1)} %bitcast.4), custom_call_target="tpu_custom_call" | custom-call | tf_op jit(solution)/shard_map/convolve/pallas_call | solution.py:398
Async XLA Ops:
  0.0 60.2 %copy-start = (f32[31,1024]{1,0:T(8,128)S(1)}, f32[31,1024]{1,0:T(8,128)}, u32[]{:S(2)}) copy-start(f32[31,1024]{1,0:T(8,128)} %taps_ref.1) | copy-start | bytes 380932
  0.0 60.2 %copy-start.1 = (f32[1024]{0:T(1024)S(1)}, f32[1024]{0:T(1024)}, u32[]{:S(2)}) copy-start(f32[1024]{0:T(1024)} %param.17) | copy-start | bytes 12292

commit v6 on v5

--- a/solution.py
+++ b/solution.py
@@ -134,22 +134,18 @@
 
     def q_copy(r):
         p = toward(r)
-        return remote(sendq.at[p], qbuf.at[r], q_send.at[r], q_recv.at[r], p * 2 + core)
+        return remote(sendq.at[p], qbuf.at[r], q_send.at[0], q_recv.at[r // 4], p * 2 + core)
 
     def kv_rows(slot, which):
         return pl.ds(pl.multiple_of((slot * 2 + which) * ROWS, ROWS), ROWS)
 
     def kv_copy(r):
         p = toward(r)
-        return remote(sendkv.at[p], kvbuf.at[kv_rows(r, core)], kv_send.at[r], kv_recv.at[r], p * 2 + core)
-
-    q_copies, kv_copies = [None] * CHIPS, [None] * CHIPS
+        return remote(sendkv.at[p], kvbuf.at[kv_rows(r, core)], kv_send.at[0], kv_recv.at[r // 4], p * 2 + core)
 
     def send(order):
         for kind, r in order:
-            copy = q_copy(r) if kind == "q" else kv_copy(r)
-            copy.start()
-            (q_copies if kind == "q" else kv_copies)[r] = copy
+            (q_copy(r) if kind == "q" else kv_copy(r)).start()
 
     own_q = pltpu.make_async_copy(sendq.at[chip], qbuf.at[0], own_sem.at[0])
     own_q.start()
@@ -172,19 +168,22 @@
     own_forward.start()
     send([("kv", r) for r in range(1, 8)] + [("q", r) for r in range(8, CHIPS)] + [("kv", r) for r in range(8, CHIPS)])
 
-    def q_arrival(slot):
-        return remote(sendq.at[0], qbuf.at[slot], q_send.at[slot], q_recv.at[slot], partner)
-
-    def kv_arrival(slot):
-        return remote(sendkv.at[0], kvbuf.at[kv_rows(slot, core)], kv_send.at[slot], kv_recv.at[slot], partner)
+    def await_q(block):
+        first = 1 if block == 0 else 0
+        group = qbuf.at[pl.ds(block * 4 + first, 4 - first)]
+        remote(group, group, q_send.at[0], q_recv.at[block], partner).wait_recv()
+
+    def await_kv(chunk):
+        group = kvbuf.at[pl.ds(chunk * BK, (3 if chunk == 0 else 4) * ROWS)]
+        remote(group, group, kv_send.at[0], kv_recv.at[chunk], partner).wait_recv()
 
     def forward(slot):
         mine = kvbuf.at[kv_rows(slot, core)]
-        return remote(mine, mine, f_send.at[slot], f_recv.at[slot], partner)
-
-    def forwarded(slot):
-        theirs = kvbuf.at[kv_rows(slot, 1 - core)]
-        return remote(theirs, theirs, f_send.at[slot], f_recv.at[slot], partner)
+        return remote(mine, mine, f_send.at[0], f_recv.at[slot // 4], partner)
+
+    def await_forwarded(chunk):
+        group = kvbuf.at[pl.ds(chunk * BK, 4 * ROWS)]
+        remote(group, group, f_send.at[0], f_recv.at[chunk], partner).wait_recv()
 
     def reset(n, carry):
         m_ref[rows_at(n, BQ), :] = jnp.full((BQ, 128), -jnp.inf, F32)
@@ -194,13 +193,12 @@
     lax.fori_loop(0, CHIPS * ROWS // BQ, reset, 0)
     own_q.wait()
     own_kv.wait()
+    await_kv(0)
     for r in range(1, 4):
-        kv_arrival(r).wait_recv()
         forward(r).start()
 
-    def unpack_q(block, skip=0):
-        for s in range(skip, 4):
-            q_arrival(block * 4 + s).wait_recv()
+    def unpack_q(block):
+        await_q(block)
         for s in range(4):
             x = qbuf[block * 4 + s].astype(F32)
             at = pl.multiple_of((block * 4 + s) * ROWS, ROWS)
@@ -208,15 +206,14 @@
             qx[pl.ds(at + HALF, HALF), :] = jnp.where(low_half, swap(x), 0.0).astype(BF16)
 
     def pass_on(chunk):
+        await_kv(chunk)
         for s in range(4):
-            kv_arrival(chunk * 4 + s).wait_recv()
             forward(chunk * 4 + s).start()
 
     low_wide = low_lanes((8 * ROWS, 128))
 
     def open_chunk(chunk):
-        for s in range(4):
-            forwarded(chunk * 4 + s).wait_recv()
+        await_forwarded(chunk)
         at = rows_at(chunk, BK)
         x = kvbuf[at, :]
         vx[at, :] = jnp.where(low_wide, jnp.ones_like(x), x)
@@ -240,8 +237,8 @@
             sendc[block * 4 + s] = jnp.where(low_half, swap(c[:HALF]), c[HALF:]).astype(BF16)
         for r in range(block * 4, block * 4 + 4):
             if r > 0:
-                remote(sendc.at[r], cbuf.at[chip], c_send.at[r], c_recv.at[r], behind(r) * 2 + core).start()
-    unpack_q(0, 1)
+                remote(sendc.at[r], cbuf.at[chip], c_send.at[0], c_recv.at[0], behind(r) * 2 + core).start()
+    unpack_q(0)
     unpack_q(1)
 
     def step(t, carry):
@@ -280,8 +277,8 @@
     for load in loads[5:]:
         load.wait()
     own_c.wait()
-    for r in range(1, CHIPS):
-        remote(sendc.at[r], cbuf.at[toward(r)], c_send.at[r], c_recv.at[r], partner).wait_recv()
+    returned = cbuf.at[pl.ds(0, CHIPS - 1)]
+    remote(returned, returned, c_send.at[0], c_recv.at[0], partner).wait_recv()
     for pair in range(HEADS // 2):
         a, b = cbuf[2 * pair].astype(F32), cbuf[2 * pair + 1].astype(F32)
         cols = slice(pair * 128, pair * 128 + 128)
@@ -311,22 +308,21 @@
     down.wait()
     padded[:, :EDGE, :] = jnp.where(ctx > 0, halos[0], 0.0)
     padded[:, EDGE + ROWS :, :] = jnp.where(ctx < 31, halos[1], 0.0)
-    own_forward.wait_send()
-    for r in range(1, CHIPS):
-        q_copies[r].wait_send()
-        kv_copies[r].wait_send()
-        forward(r).wait_send()
-        remote(sendc.at[r], cbuf.at[chip], c_send.at[r], c_recv.at[r], partner).wait_send()
-
-
-def convolve(padded_ref, mixed_ref, taps_ref, bias_ref, out_hbm, result, inner_sems, edge_sems):
+    remote(qbuf.at[pl.ds(0, CHIPS - 1)], qbuf.at[pl.ds(0, CHIPS - 1)], q_send.at[0], q_recv.at[0], partner).wait_send()
+    for sem, slots in ((kv_send, CHIPS - 1), (f_send, CHIPS)):
+        group = kvbuf.at[pl.ds(0, slots * ROWS)]
+        remote(group, group, sem.at[0], kv_recv.at[0], partner).wait_send()
+    remote(returned, returned, c_send.at[0], c_recv.at[0], partner).wait_send()
+
+
+def convolve(padded_ref, mixed_ref, taps_ref, bias_ref, out_hbm, result, sems):
     def inner(n):
         rows = pl.ds(EDGE, ROWS - 2 * EDGE)
-        return pltpu.make_async_copy(mixed_ref.at[n, rows], out_hbm.at[rows, rows_at(n, 128)], inner_sems.at[n])
+        return pltpu.make_async_copy(mixed_ref.at[n, rows], out_hbm.at[rows, rows_at(n, 128)], sems.at[0])
 
     def edge(n, side):
         rows = pl.ds(side * (ROWS - EDGE), EDGE)
-        return pltpu.make_async_copy(result.at[n, side], out_hbm.at[rows, rows_at(n, 128)], edge_sems.at[n, side])
+        return pltpu.make_async_copy(result.at[n, side], out_hbm.at[rows, rows_at(n, 128)], sems.at[1])
 
     for n in range(8):
         inner(n).start()
@@ -339,10 +335,9 @@
         return carry
 
     lax.fori_loop(0, 8, column, 0)
-    for n in range(8):
-        inner(n).wait()
-        edge(n, 0).wait()
-        edge(n, 1).wait()
+    block = mixed_ref.at[:, pl.ds(EDGE, ROWS - 2 * EDGE)]
+    pltpu.make_async_copy(block, block, sems.at[0]).wait()
+    pltpu.make_async_copy(result, result, sems.at[1]).wait()
 
 
 def per_device(frames, attend_gain, wq, wk, wv, wo, mixer_gain, depthwise, mixer_bias):
@@ -380,7 +375,7 @@
             pltpu.VMEM((KERNEL, D), F32),
             pltpu.VMEM((1, D), F32),
             dma((9,)), dma((3,)),
-            *[dma((CHIPS,))] * 8,
+            dma((1,)), dma((4,)), dma((1,)), dma((4,)), dma((1,)), dma((4,)), dma((1,)), dma((1,)),
             dma((2,)), dma((2,)),
         ],
         compiler_params=pltpu.CompilerParams(
@@ -400,7 +395,7 @@
         out_shape=jax.ShapeDtypeStruct((ROWS, D), F32),
         in_specs=[vmem] * 4,
         out_specs=hbm,
-        scratch_shapes=[pltpu.VMEM((8, 2, EDGE, 128), F32), dma((8,)), dma((8, 2))],
+        scratch_shapes=[pltpu.VMEM((8, 2, EDGE, 128), F32), dma((2,))],
         compiler_params=pltpu.CompilerParams(vmem_limit_bytes=16 * 1024 * 1024),
         name="convolve",
     )(padded, mixed, depthwise, bias)

time: 62.4 us -> 61.3 us (0.982)
  Pallas kernels: 61.6 us -> 60.3 us
    pallas_call x1, Pallas kernels: 60.2 us -> 59.2 us  [per_device(): pl.pallas_call(kernel, out_shape=(jax.ShapeDtypeStruct((8, ROWS + 2 * EDG...]
where the time goes in v6:
time: 61.3 us; the launch traced here: 60.5 us
  Pallas kernels  60.3 us (98%)
    pallas_call x1, Pallas kernels, per_device(): pl.pallas_call(kernel, out_shape=(jax.ShapeDtypeStruct((8, ROWS + 2 * EDG...  59.2 us

profile of v6, /device:TPU:16, one launch (start us, length us, event | category | flops | bytes accessed | tf_op | source)
XLA Modules:
  0.0 60.5 jit_solution(5703261605108155143)
XLA Ops:
  0.0 0.0 copy-start
  0.0 0.0 copy-start.1
  0.0 59.2 %block.1 = (f32[8,224,128]{2,1,0:T(8,128)S(1)}, f32[8,192,128]{2,1,0:T(8,128)S(1)}) custom-call(f32[192,1024]{1,0:T(8,128)} %frames_hbm.1, f32[1,1024]{1,0:T(1,128)} %bitcast.5, bf16[1024,1024]{1,0:T(8,128)(2,1)} %wq_hbm.1, bf16[1024,1024]{1,0:T(8,128)(2,1)} %wk_hbm.1, bf16[1024,1024]{1,0:T(8,128)(2,1)} %wv_hbm.1, bf16[1024,1024]{1,0:T(8,128)(2,1)} %wo_hbm.1, ...), custom_call_target="tpu_custom_call" | custom-call | tf_op jit(solution)/shard_map/block/pallas_call | solution.py:348
  59.2 0.0 copy-done
  59.2 0.0 copy-done.1
  59.2 1.2 %convolve.1 = f32[192,1024]{1,0:T(8,128)} custom-call(f32[8,224,128]{2,1,0:T(8,128)S(1)} %get-tuple-element.7.padded_ref, f32[8,192,128]{2,1,0:T(8,128)S(1)} %get-tuple-element.8.mixed_ref, f32[31,1024]{1,0:T(8,128)S(1)} %copy-done, f32[1,1024]{1,0:T(1,128)S(1)} %bitcast.4), custom_call_target="tpu_custom_call" | custom-call | tf_op jit(solution)/shard_map/convolve/pallas_call | solution.py:393
Async XLA Ops:
  0.0 59.2 %copy-start = (f32[31,1024]{1,0:T(8,128)S(1)}, f32[31,1024]{1,0:T(8,128)}, u32[]{:S(2)}) copy-start(f32[31,1024]{1,0:T(8,128)} %taps_ref.1) | copy-start | bytes 380932
  0.0 59.2 %copy-start.1 = (f32[1024]{0:T(1024)S(1)}, f32[1024]{0:T(1024)}, u32[]{:S(2)}) copy-start(f32[1024]{0:T(1024)} %param.17) | copy-start | bytes 12292

commit v7 on v6

--- a/solution.py
+++ b/solution.py
@@ -141,7 +141,7 @@
 
     def kv_copy(r):
         p = toward(r)
-        return remote(sendkv.at[p], kvbuf.at[kv_rows(r, core)], kv_send.at[0], kv_recv.at[r // 4], p * 2 + core)
+        return remote(sendkv.at[p], kvbuf.at[kv_rows(r, core)], kv_send.at[0], kv_recv.at[r // 4 if r < 12 else r - 9], p * 2 + core)
 
     def send(order):
         for kind, r in order:
@@ -206,8 +206,12 @@
             qx[pl.ds(at + HALF, HALF), :] = jnp.where(low_half, swap(x), 0.0).astype(BF16)
 
     def pass_on(chunk):
-        await_kv(chunk)
+        if chunk < 3:
+            await_kv(chunk)
         for s in range(4):
+            if chunk == 3:
+                piece = kvbuf.at[kv_rows(12 + s, core)]
+                remote(piece, piece, kv_send.at[0], kv_recv.at[3 + s], partner).wait_recv()
             forward(chunk * 4 + s).start()
 
     low_wide = low_lanes((8 * ROWS, 128))
@@ -218,24 +222,25 @@
         x = kvbuf[at, :]
         vx[at, :] = jnp.where(low_wide, jnp.ones_like(x), x)
 
-    def attend(i, j):
-        q = qx[rows_at(i, BQ), :]
+    def attend(i, j, size=BQ):
+        rows = rows_at(i, size)
+        q = qx[rows, :]
         scores = lax.dot_general(
             q, kvbuf[rows_at(j, BK), :], (((1,), (1,)), ((), ())), preferred_element_type=F32
         )
-        old = m_ref[rows_at(i, BQ), :]
+        old = m_ref[rows, :]
         new = jnp.maximum(old, jnp.max(scores, axis=1, keepdims=True))
         weights = jnp.exp2((scores - jnp.concatenate([new] * (BK // 128), axis=1)) * SCALE).astype(BF16)
         part = jnp.dot(weights, vx[rows_at(j, BK), :], preferred_element_type=F32)
-        o_ref[rows_at(i, BQ), :] = o_ref[rows_at(i, BQ), :] * jnp.exp2((old - new) * SCALE) + part
-        m_ref[rows_at(i, BQ), :] = new
-
-    def give_back(block):
-        for s in range(4):
-            o = o_ref[(block * 4 + s) * ROWS : (block * 4 + s + 1) * ROWS, :]
+        o_ref[rows, :] = o_ref[rows, :] * jnp.exp2((old - new) * SCALE) + part
+        m_ref[rows, :] = new
+
+    def give_back(slots):
+        for r in slots:
+            o = o_ref[r * ROWS : (r + 1) * ROWS, :]
             c = o / swap(o)
-            sendc[block * 4 + s] = jnp.where(low_half, swap(c[:HALF]), c[HALF:]).astype(BF16)
-        for r in range(block * 4, block * 4 + 4):
+            sendc[r] = jnp.where(low_half, swap(c[:HALF]), c[HALF:]).astype(BF16)
+        for r in slots:
             if r > 0:
                 remote(sendc.at[r], cbuf.at[chip], c_send.at[0], c_recv.at[0], behind(r) * 2 + core).start()
     unpack_q(0)
@@ -262,15 +267,16 @@
     lax.fori_loop(0, len(STEPS), step, 0)
     attend(1, 2)
     open_chunk(3)
-    attend(3, 3)
-    give_back(3)
+    for half in (6, 7):
+        attend(half, 3, 2 * ROWS)
+        give_back(range(2 * half, 2 * half + 2))
     attend(2, 3)
     attend(1, 3)
-    give_back(2)
-    give_back(1)
+    give_back(range(8, 12))
+    give_back(range(4, 8))
     attend(0, 2)
     attend(0, 3)
-    give_back(0)
+    give_back(range(4))
 
     own_c = pltpu.make_async_copy(sendc.at[0], cbuf.at[chip], own_sem.at[2])
     own_c.start()
@@ -375,7 +381,7 @@
             pltpu.VMEM((KERNEL, D), F32),
             pltpu.VMEM((1, D), F32),
             dma((9,)), dma((3,)),
-            dma((1,)), dma((4,)), dma((1,)), dma((4,)), dma((1,)), dma((4,)), dma((1,)), dma((1,)),
+            dma((1,)), dma((4,)), dma((1,)), dma((7,)), dma((1,)), dma((4,)), dma((1,)), dma((1,)),
             dma((2,)), dma((2,)),
         ],
         compiler_params=pltpu.CompilerParams(

time: 61.3 us -> 61.2 us (level)
  no operation moved by 1% of the time
where the time goes in v7:
time: 61.2 us; the launch traced here: 60 us
  Pallas kernels  59.8 us (98%)
    pallas_call x1, Pallas kernels, per_device(): pl.pallas_call(kernel, out_shape=(jax.ShapeDtypeStruct((8, ROWS + 2 * EDG...  58.6 us

profile of v7, /device:TPU:16, one launch (start us, length us, event | category | flops | bytes accessed | tf_op | source)
XLA Modules:
  0.0 60.0 jit_solution(6633807986240972079)
XLA Ops:
  0.0 0.0 copy-start
  0.0 0.0 copy-start.1
  0.0 58.6 %block.1 = (f32[8,224,128]{2,1,0:T(8,128)S(1)}, f32[8,192,128]{2,1,0:T(8,128)S(1)}) custom-call(f32[192,1024]{1,0:T(8,128)} %frames_hbm.1, f32[1,1024]{1,0:T(1,128)} %bitcast.5, bf16[1024,1024]{1,0:T(8,128)(2,1)} %wq_hbm.1, bf16[1024,1024]{1,0:T(8,128)(2,1)} %wk_hbm.1, bf16[1024,1024]{1,0:T(8,128)(2,1)} %wv_hbm.1, bf16[1024,1024]{1,0:T(8,128)(2,1)} %wo_hbm.1, ...), custom_call_target="tpu_custom_call" | custom-call | tf_op jit(solution)/shard_map/block/pallas_call | solution.py:354
  58.6 0.0 copy-done
  58.6 0.0 copy-done.1
  58.6 1.2 %convolve.1 = f32[192,1024]{1,0:T(8,128)} custom-call(f32[8,224,128]{2,1,0:T(8,128)S(1)} %get-tuple-element.7.padded_ref, f32[8,192,128]{2,1,0:T(8,128)S(1)} %get-tuple-element.8.mixed_ref, f32[31,1024]{1,0:T(8,128)S(1)} %copy-done, f32[1,1024]{1,0:T(1,128)S(1)} %bitcast.4), custom_call_target="tpu_custom_call" | custom-call | tf_op jit(solution)/shard_map/convolve/pallas_call | solution.py:399
Async XLA Ops:
  0.0 58.6 %copy-start = (f32[31,1024]{1,0:T(8,128)S(1)}, f32[31,1024]{1,0:T(8,128)}, u32[]{:S(2)}) copy-start(f32[31,1024]{1,0:T(8,128)} %taps_ref.1) | copy-start | bytes 380932
  0.0 58.6 %copy-start.1 = (f32[1024]{0:T(1024)S(1)}, f32[1024]{0:T(1024)}, u32[]{:S(2)}) copy-start(f32[1024]{0:T(1024)} %param.17) | copy-start | bytes 12292
